TPU v7x, 128 devices: a whole 4x4x4 slice. The times are simulated.
128 devices in a mesh: req: 16 (over z, x), exp: 8 (over y, core).
Axes of the slice: x: 4, y: 4, z: 4, core: 2. Of those that a mesh axis runs over, the one named last changes fastest.
Arguments:
- hidden: bfloat16 [16384, 2048], P(('req', 'exp')), may hold values from -6 to 6
- queries: bfloat16 [16384, 3072], P(('req', 'exp')), may hold values from -8 to 8
- suffix_latent: bfloat16 [16384, 576], P(('req', 'exp')), may hold values from -6 to 6
- prefix_latent: bfloat16 [16384, 576], P(('req', 'exp')), may hold values from -8 to 8
- uk_weight: bfloat16 [16, 128, 512], replicated, may hold values from -0.5 to 0.5
- uv_weight: bfloat16 [16, 512, 128], replicated, may hold values from -3 to 3
- out_weight: bfloat16 [2048, 2048], replicated, may hold values from -0.125 to 0.125
- norm_gain: float32 [2048], replicated, may hold values from 0.1 to 1.9
- expert_gate: bfloat16 [128, 2048, 704], P(('req', 'exp')), may hold values from -0.125 to 0.125
- expert_up: bfloat16 [128, 2048, 704], P(('req', 'exp')), may hold values from -0.125 to 0.125
- expert_down: bfloat16 [128, 704, 2048], P(('req', 'exp')), may hold values from -0.15625 to 0.15625
- suffix_lengths: int32 [16, 4], P('req'), may hold values from 1 to 512, 1024 in all within a row
- prefix_ids: int32 [16, 1], P('req'), may hold values from 0 to 7
- prefix_owner: int32 [16], replicated, may hold values from 0 to 15, each once
- expert_ids: int32 [16384, 6], P(('req', 'exp')), may hold values from 0 to 63, all different within a row; in each aligned block of 128 rows (0 to 127, 128 to 255, ...) at most 14 rows name the same one
- gate_weights: float32 [16384, 6], P(('req', 'exp')), may hold values from 0.1 to 0.8
Outputs:
- attended: bfloat16 [16384, 2048], P(('req', 'exp'))
- layer_out: bfloat16 [16384, 2048], P(('req', 'exp'))
Inputs may be any that keep to these rules, and one draw needn't show every extreme that they name: `suffix_lengths`: each group's 4 lengths sum to 1024. `prefix_ids`: every prefix is read by some request group. `prefix_owner`: all entries differ. `expert_ids`: a token names 6 different experts; among the 128 tokens of one device no expert is named more than 14 times.
All inputs are finite; a program needn't handle non-finite values.
Results may differ from a plain program's by a relative error of at most 0.012.
Values may be sent and summed in bfloat16 or wider, within the bound.
A program may use at most 192 MiB of HBM per device.

v0:
```python
import jax
import jax.numpy as jnp
from jax import lax
from jax.sharding import Mesh, PartitionSpec as P

EXPERTS = 64
CAP = 14


masked_score = -1e30


def request_of(positions, lengths):
    request_ends = jnp.cumsum(lengths)
    return jnp.sum((positions[:, None] >= request_ends[None, :]).astype(jnp.int32), axis=1)


def per_device(
    hidden,
    queries,
    suffix_latent,
    prefix_latent,
    uk_weight,
    uv_weight,
    out_weight,
    norm_gain,
    expert_gate,
    expert_up,
    expert_down,
    suffix_lengths,
    prefix_ids,
    prefix_owner,
    expert_ids,
    gate_weights,
):
    tok_rows = hidden.shape[0]
    head_count = uk_weight.shape[0]
    nope_width = uk_weight.shape[1]
    kv_rank = uk_weight.shape[2]
    latent_width = suffix_latent.shape[1]
    rope_width = queries.shape[1] // head_count - nope_width
    score_scale = (nope_width + rope_width) ** (-0.5)
    column = lax.axis_index("y") * lax.axis_size("core") + lax.axis_index("core")
    positions = column * tok_rows + jnp.arange(tok_rows, dtype=jnp.int32)
    lengths = suffix_lengths[0]
    own_request = request_of(positions, lengths)
    my_slot = prefix_owner[prefix_ids[0, 0]]
    q_split = queries.reshape(tok_rows, head_count, nope_width + rope_width)
    q_latent = jnp.einsum(
        "thn,hnc->thc", q_split[:, :, :nope_width], uk_weight, preferred_element_type=jnp.float32
    ).astype(jnp.bfloat16)
    q_abs = jnp.concatenate([q_latent, q_split[:, :, nope_width:]], axis=2)
    slot_chunks = lax.all_gather(prefix_latent, "req", axis=0, tiled=False)
    my_chunk = lax.dynamic_index_in_dim(slot_chunks, my_slot, 0, keepdims=False)
    both = jnp.concatenate([my_chunk, suffix_latent], axis=1)
    gathered = lax.all_gather(both, ("y", "core"), axis=0, tiled=True)
    prefix_rows = gathered[:, :latent_width]
    suffix_rows = gathered[:, latent_width:]
    key_rows = jnp.concatenate([prefix_rows, suffix_rows], axis=0)
    key_pos = jnp.arange(suffix_rows.shape[0], dtype=jnp.int32)
    key_request = request_of(key_pos, lengths)
    visible_suffix = (key_request[None, :] == own_request[:, None]) & (
        key_pos[None, :] <= positions[:, None]
    )
    visible = jnp.concatenate(
        [jnp.ones((tok_rows, prefix_rows.shape[0]), jnp.bool_), visible_suffix], axis=1
    )
    scores = (
        jnp.einsum("thc,nc->thn", q_abs, key_rows, preferred_element_type=jnp.float32) * score_scale
    )
    scores = jnp.where(visible[:, None, :], scores, masked_score)
    top_score = jnp.max(scores, axis=2, keepdims=True)
    prob_terms = jnp.where(visible[:, None, :], jnp.exp(scores - top_score), 0.0)
    weight_sum = jnp.sum(prob_terms, axis=2)
    latent_acc = jnp.einsum(
        "thn,nc->thc",
        prob_terms.astype(jnp.bfloat16),
        key_rows[:, :kv_rank],
        preferred_element_type=jnp.float32,
    )
    latent_out = (latent_acc / weight_sum[:, :, None]).astype(jnp.bfloat16)
    heads_out = jnp.einsum(
        "thc,hcv->thv", latent_out, uv_weight, preferred_element_type=jnp.float32
    ).astype(jnp.bfloat16)
    heads_out = heads_out.reshape(tok_rows, -1)
    attended = jnp.dot(heads_out, out_weight, preferred_element_type=jnp.float32).astype(
        jnp.bfloat16
    )
    residual = hidden.astype(jnp.float32) + attended.astype(jnp.float32)
    mean_square = jnp.mean(residual * residual, axis=1, keepdims=True)
    normed = (residual * lax.rsqrt(mean_square + 1e-06) * norm_gain).astype(jnp.bfloat16)
    experts = EXPERTS
    capacity = -(-CAP // 16) * 16
    top_picks = expert_ids.shape[1]
    slots = experts * capacity
    flat_ids = expert_ids.reshape(-1)
    onehot = (flat_ids[:, None] == jnp.arange(experts, dtype=jnp.int32)[None, :]).astype(jnp.int32)
    slot_rank = jnp.sum((jnp.cumsum(onehot, axis=0) - 1) * onehot, axis=1)
    target = flat_ids * capacity + slot_rank
    hits = jnp.arange(slots, dtype=jnp.int32)[None, :] == target[:, None]
    placing = hits.astype(jnp.bfloat16).reshape(tok_rows, top_picks, slots).sum(axis=1)
    packed = lax.dot_general(
        placing, normed, (((0,), (0,)), ((), ())), preferred_element_type=jnp.float32
    ).astype(jnp.bfloat16)
    width = packed.shape[1]
    recv_rows = lax.all_to_all(packed, ("req", "y"), 0, 0, tiled=True)
    chip_rows = lax.all_gather(recv_rows, "core", axis=0, tiled=True)
    gate_proj = jnp.dot(chip_rows, expert_gate[0], preferred_element_type=jnp.float32)
    up_proj = jnp.dot(chip_rows, expert_up[0], preferred_element_type=jnp.float32)
    active = (jax.nn.silu(gate_proj) * up_proj).astype(jnp.bfloat16)
    part = jnp.dot(active, expert_down[0], preferred_element_type=jnp.float32).astype(jnp.bfloat16)
    both_parts = lax.all_to_all(part, "core", 0, 0, tiled=True)
    pair_total = (
        both_parts[:slots].astype(jnp.float32) + both_parts[slots:].astype(jnp.float32)
    ).astype(jnp.bfloat16)
    returned = lax.all_to_all(pair_total, ("req", "y"), 0, 0, tiled=True)
    pick_weight = jnp.sum(
        jnp.where(hits.reshape(tok_rows, top_picks, slots), gate_weights[:, :, None], 0.0), axis=1
    )
    routed = jnp.dot(
        pick_weight,
        returned.astype(jnp.float32),
        precision=lax.Precision.HIGHEST,
        preferred_element_type=jnp.float32,
    )
    layer_out = (residual + routed).astype(jnp.bfloat16)
    return (attended, layer_out)


def solution(mesh):
    req_count = mesh.shape["req"]
    exp_count = mesh.shape["exp"]
    chip_mesh = Mesh(
        mesh.devices.reshape(req_count, exp_count // 2, 2), ("req", "y", "core")
    )
    rows = ("req", "y", "core")
    in_specs = (
        P(rows, None),
        P(rows, None),
        P(rows, None),
        P(rows, None),
        P(),
        P(),
        P(),
        P(),
        P(rows, None, None),
        P(rows, None, None),
        P(rows, None, None),
        P("req", None),
        P("req", None),
        P(),
        P(rows, None),
        P(rows, None),
    )
    out_specs = (P(rows, None), P(rows, None))
    return jax.shard_map(
        per_device, mesh=chip_mesh, in_specs=in_specs, out_specs=out_specs, check_vma=False
    )
```

profile of v0, /device:TPU:2, one launch (start us, length us, event | category | flops | bytes accessed | tf_op | source)
XLA Modules:
  0.0 331.9 jit_solution(6831687134274186519)
XLA Ops:
  8.8 1.2 dynamic_slice.7
  12.0 48.5 %all-gather.9.cloned.1.call-done = bf16[2048,576]{0,1:T(8,128)(2,1)} async-done(((bf16[128,576]{0,1:T(8,128)(2,1)}), bf16[2048,576]{0,1:T(8,128)(2,1)}) %all-gather.9.cloned.1.call-update) | async-done | bytes 2359312 | tf_op jit(solution)/shard_map/all_gather | solution.py:53
  60.5 2.4 copy.72
  64.6 2.3 copy.55
  66.9 1.0 slice.39
  67.9 1.8 reduce-window.19
  70.9 1.1 fusion.23
  72.0 3.9 %convert_bitcast_fusion = bf16[128,16,512]{0,2,1:T(8,128)(2,1)} fusion(bf16[16,128,512]{2,1,0:T(8,128)(2,1)} %param.20, bf16[128,16,192]{0,2,1:T(8,128)(2,1)} %bitcast.83), kind=kOutput, calls=%fused_computation.33 | convolution fusion | flops 269484032 | bytes 4718592 | tf_op jit(solution)/shard_map/thn,hnc->thc/dot_general | solution.py:49
  75.9 15.6 %all-gather.5.cloned.1.call-done = bf16[1024,1152]{0,1:T(8,128)(2,1)} async-done(((bf16[128,1152]{0,1:T(8,128)(2,1)}), bf16[1024,1152]{0,1:T(8,128)(2,1)}) %all-gather.5.cloned.1.call-update) | async-done | bytes 2359312 | tf_op jit(solution)/shard_map/all_gather | solution.py:56
  91.6 3.2 fusion.55
  94.8 15.9 %fusion.56 = (f32[128,16]{0,1:T(8,128)S(1)}, bf16[128,16,2048]{2,0,1:T(8,128)(2,1)}) fusion(pred[128,2048]{1,0:T(8,128)(4,1)S(1)} %concatenate.12, bf16[128,16,64]{0,2,1:T(8,128)(2,1)S(1)} %slice.39, bf16[128,16,512]{0,2,1:T(8,128)(2,1)} %convert_bitcast_fusion, bf16[1024,576]{0,1:T(8,128)(2,1)} %get-tuple-element.3, bf16[1024,576]{0,1:T(8,128)(2,1)} %get-tuple-element.2), kind=kOutput, calls=%fused_computation.70 | convolution fusion | flops 4866443264 | bytes 13377536 | tf_op jit(solution)/shard_map/sub | solution.py:73
  110.7 10.7 %fusion.34 = bf16[16,128,128]{1,2,0:T(8,128)(2,1)} fusion(bf16[16,512,128]{2,1,0:T(8,128)(2,1)} %param.21, bf16[128,16,2048]{2,0,1:T(8,128)(2,1)} %get-tuple-element.5, bf16[1024,576]{0,1:T(8,128)(2,1)} %get-tuple-element.2, bf16[1024,576]{0,1:T(8,128)(2,1)} %get-tuple-element.3, f32[128,16]{0,1:T(8,128)S(1)} %get-tuple-element.4), kind=kOutput, calls=%fused_computation.37 | convolution fusion | flops 4569956352 | bytes 13377536 | tf_op jit(solution)/shard_map/thc,hcv->thv/dot_general | solution.py:82
  121.4 5.0 %multiply_reduce_fusion = (f32[128]{0:T(128)S(1)}, bf16[128,2048]{1,0:T(8,128)(2,1)S(1)}) fusion(bf16[128,2048]{1,0:T(8,128)(2,1)S(1)} %copy-done.2, bf16[128,2048]{0,1:T(8,128)(2,1)} %bitcast.86, bf16[2048,2048]{1,0:T(8,128)(2,1)} %param.22), kind=kOutput, calls=%fused_computation.39 | convolution fusion | flops 1075314560 | bytes 9961984 | tf_op jit(solution)/shard_map/dot_general | solution.py:86
  126.4 1.4 convolution_convert_fusion.1
  127.8 61.8 %all_to_all.30 = bf16[64,16,2048]{2,1,0:T(8,128)(2,1)} all-to-all(bf16[64,16,2048]{2,1,0:T(8,128)(2,1)S(1)} %bitcast.78), channel_id=1, replica_groups=mesh['req'=16,'y'=4,'core'=2] {'req','y'}, dimensions={0} | all-to-all | bytes 8388608 | tf_op jit(solution)/shard_map/all_to_all | solution.py:106
  189.6 20.8 %all-gather.7.cloned.1.call-done = bf16[2048,2048]{1,0:T(8,128)(2,1)} async-done(((bf16[1024,2048]{1,0:T(8,128)(2,1)}), bf16[2048,2048]{1,0:T(8,128)(2,1)}) %all-gather.7.cloned.1.call-update) | async-done | bytes 8388624 | tf_op jit(solution)/shard_map/all_gather | solution.py:107
  210.4 11.0 %fusion.13 = f32[2048,704]{0,1:T(8,128)} fusion(bf16[2048,2048]{1,0:T(8,128)(2,1)} %all-gather.7.cloned.1.call-done, bf16[1,2048,704]{1,2,0:T(8,128)(2,1)} %param.24), kind=kOutput, calls=%fused_computation.20 | convolution fusion | flops 5905580032 | bytes 17039360 | tf_op jit(solution)/shard_map/dot_general | solution.py:108
  221.4 19.1 %convolution_convert_fusion = bf16[2048,2048]{1,0:T(8,128)(2,1)} fusion(f32[2048,704]{0,1:T(8,128)} %fusion.13, bf16[2048,2048]{1,0:T(8,128)(2,1)} %all-gather.7.cloned.1.call-done, bf16[1,704,2048]{2,1,0:T(8,128)(2,1)S(1)} %copy-done, bf16[1,2048,704]{1,2,0:T(8,128)(2,1)} %param.25), kind=kOutput, calls=%fused_computation.10 | convolution fusion | flops 11824005120 | bytes 28311552 | tf_op jit(solution)/shard_map/dot_general | solution.py:111
  240.5 12.1 %all_to_all.31 = bf16[2,1024,2048]{2,1,0:T(8,128)(2,1)S(1)} all-to-all(bf16[2,1024,2048]{2,1,0:T(8,128)(2,1)} %bitcast.81), channel_id=1, replica_groups=mesh['req'=16,'y'=4,'core'=2] {'core'}, dimensions={0} | all-to-all | bytes 16777216 | tf_op jit(solution)/shard_map/all_to_all | solution.py:112
  252.5 3.0 add_convert_fusion
  255.5 10.7 %all-to-all-start.2 = ((bf16[64,16,2048]{2,1,0:T(8,128)(2,1)}), bf16[64,16,2048]{2,1,0:T(8,128)(2,1)}, u32[]{:S(2)}, u32[]{:S(2)}) async-start(bf16[64,16,2048]{2,1,0:T(8,128)(2,1)} %bitcast.79), calls=%async_computation.2 | async-start | bytes 8388608 | tf_op jit(solution)/shard_map/all_to_all | solution.py:116
  266.3 1.3 select_reduce_fusion
  267.5 52.8 %all-to-all-done.2 = bf16[64,16,2048]{2,1,0:T(8,128)(2,1)} async-done(((bf16[64,16,2048]{2,1,0:T(8,128)(2,1)}), bf16[64,16,2048]{2,1,0:T(8,128)(2,1)}, u32[]{:S(2)}, u32[]{:S(2)}) %all-to-all-start.2) | async-done | bytes 4194336 | tf_op jit(solution)/shard_map/all_to_all | solution.py:116
  320.3 5.1 %fusion.16 = bf16[128,2048]{1,0:T(8,128)(2,1)} fusion(f32[128,1024]{1,0:T(8,128)} %select_reduce_fusion, bf16[1024,2048]{1,0:T(8,128)(2,1)} %bitcast.19, bf16[128,2048]{1,0:T(8,128)(2,1)} %copy-done.3, bf16[128,2048]{1,0:T(8,128)(2,1)S(1)} %copy-done.2), kind=kOutput, calls=%fused_computation.28 | convolution fusion | flops 3222536192 | bytes 6291456 | tf_op jit(solution)/shard_map/dot_general | solution.py:120
  (46 shorter events, 3.6 us)
Async XLA Ops:
  7.2 214.2 %copy-start = (bf16[1,704,2048]{2,1,0:T(8,128)(2,1)S(1)}, bf16[1,704,2048]{2,1,0:T(8,128)(2,1)}, u32[]{:S(2)}) copy-start(bf16[1,704,2048]{2,1,0:T(8,128)(2,1)} %param.26) | copy-start | bytes 8650756
  7.2 56.0 %copy-start.5 = (bf16[128,576]{0,1:T(8,128)(2,1)S(1)}, bf16[128,576]{0,1:T(8,128)(2,1)}, u32[]{:S(2)}) copy-start(bf16[128,576]{0,1:T(8,128)(2,1)} %param.18) | copy-start | bytes 442372
  7.2 56.9 %copy-start.6 = (s32[128,6]{0,1:T(8,128)S(1)}, s32[128,6]{0,1:T(8,128)}, u32[]{:S(2)}) copy-start(s32[128,6]{0,1:T(8,128)} %param.30) | copy-start | bytes 9220
  7.2 57.2 %copy-start.9 = (s32[1,4]{1,0:T(1,128)S(1)}, s32[1,4]{1,0:T(1,128)}, u32[]{:S(2)}) copy-start(s32[1,4]{1,0:T(1,128)} %param.27) | copy-start | bytes 52
  7.2 53.3 %all-gather.9.cloned.1.call-start = ((), (), s32[]{:S(2)}) async-start(), calls=%async_computation.5 | async-start | bytes 2506752 | tf_op jit(solution)/shard_map/all_gather | solution.py:53
  7.9 83.6 %all-gather.5.cloned.1.call-start = ((), (), s32[]{:S(2)}) async-start(), calls=%async_computation.3 | async-start | bytes 2654208 | tf_op jit(solution)/shard_map/all_gather | solution.py:56
  64.0 146.4 %all-gather.7.cloned.1.call-start = ((), (), s32[]{:S(2)}) async-start(), calls=%async_computation.4 | async-start | bytes 12582912 | tf_op jit(solution)/shard_map/all_gather | solution.py:107
  110.7 10.7 %copy-start.2 = (bf16[128,2048]{1,0:T(8,128)(2,1)S(1)}, bf16[128,2048]{1,0:T(8,128)(2,1)}, u32[]{:S(2)}) copy-start(bf16[128,2048]{1,0:T(8,128)(2,1)} %param.16) | copy-start | bytes 1572868
  121.4 5.0 %copy-start.4 = (bf16[128,1024]{1,0:T(8,128)(2,1)S(1)}, bf16[128,1024]{1,0:T(8,128)(2,1)}, u32[]{:S(2)}) copy-start(bf16[128,1024]{1,0:T(8,128)(2,1)} %fusion.23) | copy-start | bytes 786436
  121.4 5.0 %copy-start.7 = (f32[2048]{0:T(1024)S(1)}, f32[2048]{0:T(1024)}, u32[]{:S(2)}) copy-start(f32[2048]{0:T(1024)} %param.23) | copy-start | bytes 24580
  126.3 1.4 copy-start.3
  255.5 10.7 %copy-start.8 = (f32[128,6]{0,1:T(8,128)S(1)}, f32[128,6]{0,1:T(8,128)}, u32[]{:S(2)}) copy-start(f32[128,6]{0,1:T(8,128)} %param.31) | copy-start | bytes 9220
  255.5 64.8 %all-to-all-start.2 = ((bf16[64,16,2048]{2,1,0:T(8,128)(2,1)}), bf16[64,16,2048]{2,1,0:T(8,128)(2,1)}, u32[]{:S(2)}, u32[]{:S(2)}) async-start(bf16[64,16,2048]{2,1,0:T(8,128)(2,1)} %bitcast.79), calls=%async_computation.2 | async-start | bytes 8388608 | tf_op jit(solution)/shard_map/all_to_all | solution.py:116
  266.2 59.2 %copy-start.1 = (bf16[1,704,2048]{2,1,0:T(8,128)(2,1)S(1)}, bf16[1,704,2048]{2,1,0:T(8,128)(2,1)}, u32[]{:S(2)}) copy-start(bf16[1,704,2048]{2,1,0:T(8,128)(2,1)} %param.26) | copy-start | bytes 8650756
Sparse Core Ops, SparseCore 0:
  10.1 50.3 all-gather.8
  64.1 27.4 all-gather.4
  189.7 20.6 all-gather.6
where the time goes:
time: 333 us; the launch traced here: 332 us
  waiting for transfers between devices  138 us (41%)
  blocking collectives  73.9 us (22%)
  matrix products  72 us (22%)
  between operations  16.7 us (5%)
  local copies, waits for them, and re-layouts  11.4 us (3%)
  starting transfers between devices  10.8 us (3%)
  other arithmetic  8.65 us (3%)
    all_to_all x1, blocking collectives, per_device(): recv_rows = lax.all_to_all(packed, ('req', 'y'), 0, 0, tiled=True)  61.8 us
    all_to_all x1, waiting for transfers between devices, per_device(): returned = lax.all_to_all(pair_total, ('req', 'y'), 0, 0, tiled=True)  52.8 us
    all_gather x1, waiting for transfers between devices, per_device(): slot_chunks = lax.all_gather(prefix_latent, 'req', axis=0, tiled=False)  48.5 us
    all_gather x1, waiting for transfers between devices, per_device(): chip_rows = lax.all_gather(recv_rows, 'core', axis=0, tiled=True)  20.8 us
    dot_general x1, matrix products, per_device(): jnp.dot(active, expert_down[0], preferred_element_type=jnp.float32)  19.1 us
    sub x1, matrix products, per_device(): scores - top_score  15.9 us
    all_gather x1, waiting for transfers between devices, per_device(): gathered = lax.all_gather(both, ('y', 'core'), axis=0, tiled=True)  15.6 us
    all_to_all x1, blocking collectives, per_device(): both_parts = lax.all_to_all(part, 'core', 0, 0, tiled=True)  12.1 us
  transfers between devices with their start and end apart: 4, of which 4 were waited for; matrix products, arithmetic and copies ran while one was open for 4% of the time, Pallas kernels for 0%

commit v1 on v0

--- a/solution.py
+++ b/solution.py
@@ -15,7 +15,7 @@
     return jnp.sum((positions[:, None] >= request_ends[None, :]).astype(jnp.int32), axis=1)
 
 
-def per_device(
+def layer(
     hidden,
     queries,
     suffix_latent,
@@ -66,7 +66,8 @@
         [jnp.ones((tok_rows, prefix_rows.shape[0]), jnp.bool_), visible_suffix], axis=1
     )
     scores = (
-        jnp.einsum("thc,nc->thn", q_abs, key_rows, preferred_element_type=jnp.float32) * score_scale
+        jnp.einsum("thc,nc->thn", q_abs, key_rows, preferred_element_type=jnp.float32)
+        * score_scale
     )
     scores = jnp.where(visible[:, None, :], scores, masked_score)
     top_score = jnp.max(scores, axis=2, keepdims=True)
@@ -102,17 +103,23 @@
     packed = lax.dot_general(
         placing, normed, (((0,), (0,)), ((), ())), preferred_element_type=jnp.float32
     ).astype(jnp.bfloat16)
-    width = packed.shape[1]
+    swap = [(0, 1), (1, 0)]
+    sibling_gate = lax.ppermute(expert_gate, "core", swap)
+    sibling_up = lax.ppermute(expert_up, "core", swap)
+    sibling_down = lax.ppermute(expert_down, "core", swap)
     recv_rows = lax.all_to_all(packed, ("req", "y"), 0, 0, tiled=True)
-    chip_rows = lax.all_gather(recv_rows, "core", axis=0, tiled=True)
-    gate_proj = jnp.dot(chip_rows, expert_gate[0], preferred_element_type=jnp.float32)
-    up_proj = jnp.dot(chip_rows, expert_up[0], preferred_element_type=jnp.float32)
-    active = (jax.nn.silu(gate_proj) * up_proj).astype(jnp.bfloat16)
-    part = jnp.dot(active, expert_down[0], preferred_element_type=jnp.float32).astype(jnp.bfloat16)
-    both_parts = lax.all_to_all(part, "core", 0, 0, tiled=True)
-    pair_total = (
-        both_parts[:slots].astype(jnp.float32) + both_parts[slots:].astype(jnp.float32)
-    ).astype(jnp.bfloat16)
+
+    def half_expert(gate_w, up_w, down_w):
+        gate_proj = jnp.dot(recv_rows, gate_w, preferred_element_type=jnp.float32)
+        up_proj = jnp.dot(recv_rows, up_w, preferred_element_type=jnp.float32)
+        active = (jax.nn.silu(gate_proj) * up_proj).astype(jnp.bfloat16)
+        return jnp.dot(active, down_w, preferred_element_type=jnp.float32).astype(jnp.bfloat16)
+
+    own_part = half_expert(expert_gate[0], expert_up[0], expert_down[0])
+    sibling_part = half_expert(sibling_gate[0], sibling_up[0], sibling_down[0])
+    pair_total = (own_part.astype(jnp.float32) + sibling_part.astype(jnp.float32)).astype(
+        jnp.bfloat16
+    )
     returned = lax.all_to_all(pair_total, ("req", "y"), 0, 0, tiled=True)
     pick_weight = jnp.sum(
         jnp.where(hits.reshape(tok_rows, top_picks, slots), gate_weights[:, :, None], 0.0), axis=1
@@ -154,5 +161,5 @@
     )
     out_specs = (P(rows, None), P(rows, None))
     return jax.shard_map(
-        per_device, mesh=chip_mesh, in_specs=in_specs, out_specs=out_specs, check_vma=False
+        layer, mesh=chip_mesh, in_specs=in_specs, out_specs=out_specs, check_vma=False
     )

time: 333 us -> 308 us (0.925)
  blocking collectives: 73.9 us -> 0 us
  waiting for transfers between devices: 138 us -> 174 us
  matrix products: 72 us -> 81.9 us
  starting transfers between devices: 10.8 us -> 19 us
  other arithmetic: 8.65 us -> 4.95 us
    all_to_all x2 -> x0, blocking collectives: 73.9 us -> none  [the longest x1 61.8 us: per_device(): recv_rows = lax.all_to_all(packed, ('req', 'y'), 0, 0, tiled=True)]
    all_to_all x1 -> x2, waiting for transfers between devices: 52.8 us -> 106 us  [the longest x1 52.9 us: layer(): recv_rows = lax.all_to_all(packed, ('req', 'y'), 0, 0, tiled=True)]
    all_gather x3 -> x2, waiting for transfers between devices: 85 us -> 67.7 us  [the longest x1 48.6 us: layer(): slot_chunks = lax.all_gather(prefix_latent, 'req', axis=0, tiled=False)]
    dot_general x7 -> x9, matrix products: 56.2 us -> 66.2 us  [the longest x2 25.4 us: half_expert(): jnp.dot(active, down_w, preferred_element_type=jnp.float32)]
    all_to_all x1 -> x2, starting transfers between devices: 10.7 us -> 18.2 us  [the longest x1 10.3 us: layer(): recv_rows = lax.all_to_all(packed, ('req', 'y'), 0, 0, tiled=True)]
  transfers between devices with their start and end apart: 4 -> 7, of which waited for: 4 -> 4; matrix products, arithmetic and copies ran while one was open for 4% -> 13% of each run, Pallas kernels for 0% -> 0%
where the time goes in v1:
time: 308 us; the launch traced here: 307 us
  waiting for transfers between devices  174 us (56%)
  matrix products  81.9 us (27%)
  starting transfers between devices  19 us (6%)
  between operations  16.9 us (5%)
  local copies, waits for them, and re-layouts  10.4 us (3%)
  other arithmetic  4.95 us (2%)
    all_to_all x1, waiting for transfers between devices, layer(): recv_rows = lax.all_to_all(packed, ('req', 'y'), 0, 0, tiled=True)  52.9 us
    all_to_all x1, waiting for transfers between devices, layer(): returned = lax.all_to_all(pair_total, ('req', 'y'), 0, 0, tiled=True)  52.9 us
    all_gather x1, waiting for transfers between devices, layer(): slot_chunks = lax.all_gather(prefix_latent, 'req', axis=0, tiled=False)  48.6 us
    dot_general x2, matrix products, half_expert(): jnp.dot(active, down_w, preferred_element_type=jnp.float32)  25.4 us
    all_gather x1, waiting for transfers between devices, layer(): gathered = lax.all_gather(both, ('y', 'core'), axis=0, tiled=True)  19.1 us
    dot_general x2, matrix products, half_expert(): up_proj = jnp.dot(recv_rows, up_w, preferred_element_type=jnp.float32)  15.7 us
    sub x1, matrix products, layer(): scores - top_score  15.6 us
    all_to_all x1, starting transfers between devices, layer(): recv_rows = lax.all_to_all(packed, ('req', 'y'), 0, 0, tiled=True)  10.3 us
  transfers between devices with their start and end apart: 7, of which 4 were waited for; matrix products, arithmetic and copies ran while one was open for 13% of the time, Pallas kernels for 0%

profile of v1, /device:TPU:2, one launch (start us, length us, event | category | flops | bytes accessed | tf_op | source)
XLA Modules:
  0.0 307.4 jit_solution(14071836374858082260)
XLA Ops:
  8.6 1.3 dynamic_slice.7
  11.8 48.6 %all-gather.6.cloned.1.call-done = bf16[2048,576]{0,1:T(8,128)(2,1)} async-done(((bf16[128,576]{0,1:T(8,128)(2,1)}), bf16[2048,576]{0,1:T(8,128)(2,1)}) %all-gather.6.cloned.1.call-update) | async-done | bytes 2359312 | tf_op jit(solution)/shard_map/all_gather | solution.py:53
  60.5 2.4 copy.72
  63.2 0.7 pad_maximum_fusion.8
  64.6 1.5 copy.55
  66.1 0.7 slice.29
  66.8 1.8 reduce-window.19
  70.2 2.2 convert_bitcast_fusion
  72.4 19.1 %all-gather.4.cloned.1.call-done = bf16[1024,1152]{0,1:T(8,128)(2,1)} async-done(((bf16[128,1152]{0,1:T(8,128)(2,1)}), bf16[1024,1152]{0,1:T(8,128)(2,1)}) %all-gather.4.cloned.1.call-update) | async-done | bytes 2359312 | tf_op jit(solution)/shard_map/all_gather | solution.py:56
  91.5 3.2 %fusion.70 = (bf16[1024,576]{0,1:T(8,128)(2,1)}, bf16[1024,576]{0,1:T(8,128)(2,1)}) fusion(bf16[1024,1152]{0,1:T(8,128)(2,1)} %all-gather.4.cloned.1.call-done), kind=kLoop, calls=%fused_computation.77 | loop fusion | bytes 4718592 | tf_op jit(solution)/shard_map/slice | solution.py:57
  94.8 15.6 %fusion.71 = (f32[128,16]{0,1:T(8,128)S(1)}, bf16[128,16,2048]{2,0,1:T(8,128)(2,1)}) fusion(pred[128,2048]{1,0:T(8,128)(4,1)S(1)} %concatenate.12, bf16[128,16,64]{0,2,1:T(8,128)(2,1)S(1)} %copy-done.5, bf16[128,16,512]{0,2,1:T(8,128)(2,1)S(1)} %copy-done.4, bf16[1024,576]{0,1:T(8,128)(2,1)} %get-tuple-element.3, bf16[1024,576]{0,1:T(8,128)(2,1)} %get-tuple-element.2), kind=kOutput, calls=%fused_computation.78 | convolution fusion | flops 4866443264 | bytes 13377536 | tf_op jit(solution)/shard_map/sub | solution.py:74
  110.4 9.9 %fusion.42 = bf16[16,128,128]{1,2,0:T(8,128)(2,1)S(1)} fusion(bf16[16,512,128]{2,1,0:T(8,128)(2,1)} %param.21, bf16[128,16,2048]{2,0,1:T(8,128)(2,1)} %get-tuple-element.5, bf16[1024,576]{0,1:T(8,128)(2,1)} %get-tuple-element.2, bf16[1024,576]{0,1:T(8,128)(2,1)} %get-tuple-element.3, f32[128,16]{0,1:T(8,128)S(1)} %get-tuple-element.4), kind=kOutput, calls=%fused_computation.44 | convolution fusion | flops 4569956352 | bytes 13377536 | tf_op jit(solution)/shard_map/thc,hcv->thv/dot_general | solution.py:83
  120.3 4.8 %multiply_reduce_fusion = (f32[128]{0:T(128)S(1)}, bf16[128,2048]{1,0:T(8,128)(2,1)S(1)}) fusion(bf16[128,2048]{1,0:T(8,128)(2,1)S(1)} %copy-done.2, bf16[128,2048]{0,1:T(8,128)(2,1)S(1)} %bitcast.101, bf16[2048,2048]{1,0:T(8,128)(2,1)} %param.22), kind=kOutput, calls=%fused_computation.46 | convolution fusion | flops 1075314560 | bytes 9961984 | tf_op jit(solution)/shard_map/dot_general | solution.py:87
  125.1 3.3 %convolution_convert_fusion = bf16[1024,2048]{1,0:T(8,128)(2,1)} fusion(bf16[128,1024]{1,0:T(8,128)(2,1)S(1)} %fusion.30, bf16[128,2048]{1,0:T(8,128)(2,1)S(1)} %get-tuple-element.7, bf16[128,2048]{1,0:T(8,128)(2,1)S(1)} %copy-done.2, f32[2048]{0:T(1024)S(1)} %copy-done.8, f32[128]{0:T(128)S(1)} %add_rsqrt_fusion), kind=kOutput, calls=%fused_computation.12 | convolution fusion | flops 540540928 | bytes 5513728 | tf_op jit(solution)/shard_map/dot_general | solution.py:103
  128.4 10.3 %all-to-all-start = ((bf16[64,16,2048]{2,1,0:T(8,128)(2,1)}), bf16[64,16,2048]{2,1,0:T(8,128)(2,1)}, u32[]{:S(2)}, u32[]{:S(2)}) async-start(bf16[64,16,2048]{2,1,0:T(8,128)(2,1)} %bitcast.95), calls=%async_computation | async-start | bytes 8388608 | tf_op jit(solution)/shard_map/all_to_all | solution.py:110
  139.3 52.9 %all-to-all-done = bf16[64,16,2048]{2,1,0:T(8,128)(2,1)} async-done(((bf16[64,16,2048]{2,1,0:T(8,128)(2,1)}), bf16[64,16,2048]{2,1,0:T(8,128)(2,1)}, u32[]{:S(2)}, u32[]{:S(2)}) %all-to-all-start) | async-done | bytes 4194336 | tf_op jit(solution)/shard_map/all_to_all | solution.py:110
  192.2 7.8 %fusion.17 = f32[1024,704]{0,1:T(8,128)} fusion(bf16[1024,2048]{1,0:T(8,128)(2,1)} %bitcast.13, bf16[1,2048,704]{1,2,0:T(8,128)(2,1)} %param.25), kind=kOutput, calls=%fused_computation.23 | convolution fusion | flops 2952790016 | bytes 9961472 | tf_op jit(solution)/shard_map/dot_general | solution.py:114
  200.1 7.8 %fusion.11 = f32[1024,704]{0,1:T(8,128)} fusion(bf16[1024,2048]{1,0:T(8,128)(2,1)} %bitcast.13, bf16[1,2048,704]{1,2,0:T(8,128)(2,1)} %collective-permute-done.1), kind=kOutput, calls=%fused_computation.17 | convolution fusion | flops 2952790016 | bytes 9961472 | tf_op jit(solution)/shard_map/dot_general | solution.py:114
  207.9 12.2 %fusion.15 = bf16[1024,2048]{1,0:T(8,128)(2,1)} fusion(bf16[1,704,2048]{2,1,0:T(8,128)(2,1)} %param.26, f32[1024,704]{0,1:T(8,128)} %fusion.17, bf16[1024,2048]{1,0:T(8,128)(2,1)} %bitcast.13, bf16[1,2048,704]{1,2,0:T(8,128)(2,1)} %param.24), kind=kOutput, calls=%fused_computation.21 | convolution fusion | flops 5909905408 | bytes 17039360 | tf_op jit(solution)/shard_map/dot_general | solution.py:116
  220.1 13.2 %add_convert_fusion = bf16[1024,2048]{1,0:T(8,128)(2,1)} fusion(bf16[1024,2048]{1,0:T(8,128)(2,1)} %fusion.15, bf16[1,704,2048]{2,1,0:T(8,128)(2,1)} %collective-permute-done.2, f32[1024,704]{0,1:T(8,128)} %fusion.11, bf16[1024,2048]{1,0:T(8,128)(2,1)} %bitcast.13, bf16[1,2048,704]{1,2,0:T(8,128)(2,1)} %collective-permute-done), kind=kOutput, calls=%fused_computation.4 | convolution fusion | flops 5920391168 | bytes 21233664 | tf_op jit(solution)/shard_map/dot_general | solution.py:116
  233.3 8.0 %all-to-all-start.1 = ((bf16[64,16,2048]{2,1,0:T(8,128)(2,1)}), bf16[64,16,2048]{2,1,0:T(8,128)(2,1)}, u32[]{:S(2)}, u32[]{:S(2)}) async-start(bf16[64,16,2048]{2,1,0:T(8,128)(2,1)} %bitcast.96), calls=%async_computation.1 | async-start | bytes 8388608 | tf_op jit(solution)/shard_map/all_to_all | solution.py:123
  241.3 1.2 select_reduce_fusion
  242.5 52.9 %all-to-all-done.1 = bf16[64,16,2048]{2,1,0:T(8,128)(2,1)} async-done(((bf16[64,16,2048]{2,1,0:T(8,128)(2,1)}), bf16[64,16,2048]{2,1,0:T(8,128)(2,1)}, u32[]{:S(2)}, u32[]{:S(2)}) %all-to-all-start.1) | async-done | bytes 4194336 | tf_op jit(solution)/shard_map/all_to_all | solution.py:123
  295.4 5.1 %fusion.21 = bf16[128,2048]{1,0:T(8,128)(2,1)} fusion(f32[128,1024]{1,0:T(8,128)} %select_reduce_fusion, bf16[1024,2048]{1,0:T(8,128)(2,1)} %bitcast.21, bf16[128,2048]{1,0:T(8,128)(2,1)S(1)} %get-tuple-element.7, bf16[128,2048]{1,0:T(8,128)(2,1)S(1)} %copy-done.2), kind=kOutput, calls=%fused_computation.34 | convolution fusion | flops 3222536192 | bytes 6291456 | tf_op jit(solution)/shard_map/dot_general | solution.py:127
  (52 shorter events, 4.0 us)
Async XLA Ops:
  7.2 63.1 %copy-start = (bf16[16,128,512]{2,1,0:T(8,128)(2,1)S(1)}, bf16[16,128,512]{2,1,0:T(8,128)(2,1)}, u32[]{:S(2)}) copy-start(bf16[16,128,512]{2,1,0:T(8,128)(2,1)} %param.20) | copy-start | bytes 6291460
  7.2 53.3 %all-gather.6.cloned.1.call-start = ((), (), s32[]{:S(2)}) async-start(), calls=%async_computation.3 | async-start | bytes 2506752 | tf_op jit(solution)/shard_map/all_gather | solution.py:53
  7.9 83.6 %all-gather.4.cloned.1.call-start = ((), (), s32[]{:S(2)}) async-start(), calls=%async_computation.2 | async-start | bytes 2654208 | tf_op jit(solution)/shard_map/all_gather | solution.py:56
  8.6 54.6 %copy-start.6 = (bf16[128,576]{0,1:T(8,128)(2,1)S(1)}, bf16[128,576]{0,1:T(8,128)(2,1)}, u32[]{:S(2)}) copy-start(bf16[128,576]{0,1:T(8,128)(2,1)} %param.18) | copy-start | bytes 442372
  60.5 3.5 %copy-start.7 = (s32[128,6]{0,1:T(8,128)S(1)}, s32[128,6]{0,1:T(8,128)}, u32[]{:S(2)}) copy-start(s32[128,6]{0,1:T(8,128)} %param.30) | copy-start | bytes 9220
  60.5 3.9 %copy-start.10 = (s32[1,4]{1,0:T(1,128)S(1)}, s32[1,4]{1,0:T(1,128)}, u32[]{:S(2)}) copy-start(s32[1,4]{1,0:T(1,128)} %param.27) | copy-start | bytes 52
  72.4 22.4 %copy-start.4 = (bf16[128,16,512]{0,2,1:T(8,128)(2,1)S(1)}, bf16[128,16,512]{0,2,1:T(8,128)(2,1)}, u32[]{:S(2)}) copy-start(bf16[128,16,512]{0,2,1:T(8,128)(2,1)} %convert_bitcast_fusion) | copy-start | bytes 6291460
  72.4 22.4 %copy-start.5 = (bf16[128,16,64]{0,2,1:T(8,128)(2,1)S(1)}, bf16[128,16,64]{0,2,1:T(8,128)(2,1)}, u32[]{:S(2)}) copy-start(bf16[128,16,64]{0,2,1:T(8,128)(2,1)} %slice.29) | copy-start | bytes 786436
  110.4 9.9 %copy-start.2 = (bf16[128,2048]{1,0:T(8,128)(2,1)S(1)}, bf16[128,2048]{1,0:T(8,128)(2,1)}, u32[]{:S(2)}) copy-start(bf16[128,2048]{1,0:T(8,128)(2,1)} %param.16) | copy-start | bytes 1572868
  120.3 4.8 %copy-start.8 = (f32[2048]{0:T(1024)S(1)}, f32[2048]{0:T(1024)}, u32[]{:S(2)}) copy-start(f32[2048]{0:T(1024)} %param.23) | copy-start | bytes 24580
  125.1 170.3 %copy-start.3 = (bf16[128,2048]{1,0:T(8,128)(2,1)}, bf16[128,2048]{1,0:T(8,128)(2,1)S(1)}, u32[]{:S(2)}) copy-start(bf16[128,2048]{1,0:T(8,128)(2,1)S(1)} %get-tuple-element.7) | copy-start | bytes 1572868
  128.4 63.9 %all-to-all-start = ((bf16[64,16,2048]{2,1,0:T(8,128)(2,1)}), bf16[64,16,2048]{2,1,0:T(8,128)(2,1)}, u32[]{:S(2)}, u32[]{:S(2)}) async-start(bf16[64,16,2048]{2,1,0:T(8,128)(2,1)} %bitcast.95), calls=%async_computation | async-start | bytes 8388608 | tf_op jit(solution)/shard_map/all_to_all | solution.py:110
  138.6 61.5 %collective-permute-start.1 = (bf16[1,2048,704]{1,2,0:T(8,128)(2,1)}, bf16[1,2048,704]{1,2,0:T(8,128)(2,1)}, u32[]{:S(2)}, u32[]{:S(2)}) collective-permute-start(bf16[1,2048,704]{1,2,0:T(8,128)(2,1)} %param.25), channel_id=1, source_target_pairs={{0,1},{1,0},{2,3},{3,2},{4,5},{5,4},{6,7},{7,6},{8,9},{9,8},{10,11... | collective-permute-start | bytes 8650760 | tf_op jit(solution)/shard_map/ppermute | solution.py:108
  138.7 81.3 %collective-permute-start = (bf16[1,2048,704]{1,2,0:T(8,128)(2,1)}, bf16[1,2048,704]{1,2,0:T(8,128)(2,1)}, u32[]{:S(2)}, u32[]{:S(2)}) collective-permute-start(bf16[1,2048,704]{1,2,0:T(8,128)(2,1)} %param.24), channel_id=1, source_target_pairs={{0,1},{1,0},{2,3},{3,2},{4,5},{5,4},{6,7},{7,6},{8,9},{9,8},{10,11... | collective-permute-start | bytes 8650760 | tf_op jit(solution)/shard_map/ppermute | solution.py:107
  139.2 80.9 %collective-permute-start.2 = (bf16[1,704,2048]{2,1,0:T(8,128)(2,1)}, bf16[1,704,2048]{2,1,0:T(8,128)(2,1)}, u32[]{:S(2)}, u32[]{:S(2)}) collective-permute-start(bf16[1,704,2048]{2,1,0:T(8,128)(2,1)} %param.26), channel_id=1, source_target_pairs={{0,1},{1,0},{2,3},{3,2},{4,5},{5,4},{6,7},{7,6},{8,9},{9,8},{10,11... | collective-permute-start | bytes 8650760 | tf_op jit(solution)/shard_map/ppermute | solution.py:109
  233.3 8.0 %copy-start.9 = (f32[128,6]{0,1:T(8,128)S(1)}, f32[128,6]{0,1:T(8,128)}, u32[]{:S(2)}) copy-start(f32[128,6]{0,1:T(8,128)} %param.31) | copy-start | bytes 9220
  233.3 62.1 %all-to-all-start.1 = ((bf16[64,16,2048]{2,1,0:T(8,128)(2,1)}), bf16[64,16,2048]{2,1,0:T(8,128)(2,1)}, u32[]{:S(2)}, u32[]{:S(2)}) async-start(bf16[64,16,2048]{2,1,0:T(8,128)(2,1)} %bitcast.96), calls=%async_computation.1 | async-start | bytes 8388608 | tf_op jit(solution)/shard_map/all_to_all | solution.py:123
  295.4 5.2 %copy-start.1 = (bf16[16,128,512]{2,1,0:T(8,128)(2,1)S(1)}, bf16[16,128,512]{2,1,0:T(8,128)(2,1)}, u32[]{:S(2)}) copy-start(bf16[16,128,512]{2,1,0:T(8,128)(2,1)} %param.20) | copy-start | bytes 6291460
Sparse Core Ops, SparseCore 0:
  10.1 50.3 all-gather.5
  64.1 27.3 all-gather.3

commit v2 on v1

--- a/solution.py
+++ b/solution.py
@@ -44,14 +44,22 @@
     positions = column * tok_rows + jnp.arange(tok_rows, dtype=jnp.int32)
     lengths = suffix_lengths[0]
     own_request = request_of(positions, lengths)
-    my_slot = prefix_owner[prefix_ids[0, 0]]
+    my_group = lax.axis_index("z") * lax.axis_size("x") + lax.axis_index("x")
+    my_slot = prefix_owner[prefix_ids[my_group, 0]]
     q_split = queries.reshape(tok_rows, head_count, nope_width + rope_width)
     q_latent = jnp.einsum(
         "thn,hnc->thc", q_split[:, :, :nope_width], uk_weight, preferred_element_type=jnp.float32
     ).astype(jnp.bfloat16)
     q_abs = jnp.concatenate([q_latent, q_split[:, :, nope_width:]], axis=2)
-    slot_chunks = lax.all_gather(prefix_latent, "req", axis=0, tiled=False)
-    my_chunk = lax.dynamic_index_in_dim(slot_chunks, my_slot, 0, keepdims=False)
+    x_count = lax.axis_size("x")
+    z_count = lax.axis_size("z")
+    my_x = lax.axis_index("x")
+    group_slots = prefix_owner[prefix_ids[:, 0]]
+    x_chunks = lax.all_gather(prefix_latent, "x", axis=0, tiled=False)
+    dest_slots = group_slots.reshape(z_count, x_count)[:, my_x]
+    sent = jnp.take(x_chunks, dest_slots % x_count, axis=0)
+    recv_chunks = lax.all_to_all(sent, "z", 0, 0, tiled=True)
+    my_chunk = lax.dynamic_index_in_dim(recv_chunks, my_slot // x_count, 0, keepdims=False)
     both = jnp.concatenate([my_chunk, suffix_latent], axis=1)
     gathered = lax.all_gather(both, ("y", "core"), axis=0, tiled=True)
     prefix_rows = gathered[:, :latent_width]
@@ -107,7 +115,7 @@
     sibling_gate = lax.ppermute(expert_gate, "core", swap)
     sibling_up = lax.ppermute(expert_up, "core", swap)
     sibling_down = lax.ppermute(expert_down, "core", swap)
-    recv_rows = lax.all_to_all(packed, ("req", "y"), 0, 0, tiled=True)
+    recv_rows = lax.all_to_all(packed, ("z", "x", "y"), 0, 0, tiled=True)
 
     def half_expert(gate_w, up_w, down_w):
         gate_proj = jnp.dot(recv_rows, gate_w, preferred_element_type=jnp.float32)
@@ -120,7 +128,7 @@
     pair_total = (own_part.astype(jnp.float32) + sibling_part.astype(jnp.float32)).astype(
         jnp.bfloat16
     )
-    returned = lax.all_to_all(pair_total, ("req", "y"), 0, 0, tiled=True)
+    returned = lax.all_to_all(pair_total, ("z", "x", "y"), 0, 0, tiled=True)
     pick_weight = jnp.sum(
         jnp.where(hits.reshape(tok_rows, top_picks, slots), gate_weights[:, :, None], 0.0), axis=1
     )
@@ -137,10 +145,13 @@
 def solution(mesh):
     req_count = mesh.shape["req"]
     exp_count = mesh.shape["exp"]
+    x_count = 4
     chip_mesh = Mesh(
-        mesh.devices.reshape(req_count, exp_count // 2, 2), ("req", "y", "core")
+        mesh.devices.reshape(req_count // x_count, x_count, exp_count // 2, 2),
+        ("z", "x", "y", "core"),
     )
-    rows = ("req", "y", "core")
+    rows = ("z", "x", "y", "core")
+    groups = ("z", "x")
     in_specs = (
         P(rows, None),
         P(rows, None),
@@ -153,8 +164,8 @@
         P(rows, None, None),
         P(rows, None, None),
         P(rows, None, None),
-        P("req", None),
-        P("req", None),
+        P(groups, None),
+        P(),
         P(),
         P(rows, None),
         P(rows, None),

time: 308 us -> 300 us (0.974)
  waiting for transfers between devices: 174 us -> 127 us
  blocking collectives: 0 us -> 30.7 us
  starting transfers between devices: 19 us -> 22.4 us
    all_gather x1 -> x0, waiting for transfers between devices: 48.6 us -> none  [layer(): slot_chunks = lax.all_gather(prefix_latent, 'req', axis=0, tiled=False)]
    unnamed x0 -> x1, blocking collectives: none -> 16.7 us
    all_gather x0 -> x1, blocking collectives: none -> 14 us  [layer(): x_chunks = lax.all_gather(prefix_latent, 'x', axis=0, tiled=False)]
    all_to_all x2 -> x3, starting transfers between devices: 18.2 us -> 21.7 us  [the longest x1 10.3 us: layer(): recv_rows = lax.all_to_all(packed, ('z', 'x', 'y'), 0, 0, tiled=True)]
    all_to_all x2 -> x3, waiting for transfers between devices: 106 us -> 108 us  [the longest x1 52.9 us: layer(): recv_rows = lax.all_to_all(packed, ('z', 'x', 'y'), 0, 0, tiled=True)]
where the time goes in v2:
time: 300 us
  waiting for transfers between devices  127 us (42%)
  matrix products  81.9 us (27%)
  blocking collectives  30.7 us (10%)
  starting transfers between devices  22.4 us (7%)
  between operations  19.7 us (7%)
  local copies, waits for them, and re-layouts  11.7 us (4%)
  other arithmetic  6.22 us (2%)
    all_to_all x1, waiting for transfers between devices, layer(): recv_rows = lax.all_to_all(packed, ('z', 'x', 'y'), 0, 0, tiled=True)  52.9 us
    all_to_all x1, waiting for transfers between devices, layer(): returned = lax.all_to_all(pair_total, ('z', 'x', 'y'), 0, 0, tiled=True)  52.7 us
    dot_general x2, matrix products, half_expert(): jnp.dot(active, down_w, preferred_element_type=jnp.float32)  25.4 us
    all_gather x1, waiting for transfers between devices, layer(): gathered = lax.all_gather(both, ('y', 'core'), axis=0, tiled=True)  19 us
    unnamed x1, blocking collectives  16.7 us
    dot_general x2, matrix products, half_expert(): up_proj = jnp.dot(recv_rows, up_w, preferred_element_type=jnp.float32)  15.6 us
    sub x1, matrix products, layer(): scores - top_score  15.6 us
    all_gather x1, blocking collectives, layer(): x_chunks = lax.all_gather(prefix_latent, 'x', axis=0, tiled=False)  14 us
  transfers between devices with their start and end apart: 7, of which 4 were waited for; matrix products, arithmetic and copies ran while one was open for 13% of the time, Pallas kernels for 0%

profile of v2, /device:TPU:2, one launch (start us, length us, event | category | flops | bytes accessed | tf_op | source)
XLA Modules:
  0.0 299.8 jit_solution(14194994802874975180)
XLA Ops:
  8.0 1.2 dynamic-slice
  9.9 16.7 %all-reduce.1 = s32[16]{0:T(128)S(1)} all-reduce(s32[16]{0:T(128)S(1)} %bitcast_dynamic-update-slice_fusion), channel_id=3, replica_groups=mesh['z'=4,'x'=4,'y'=4,'core'=2] {'z','x'}, use_global_device_ids=true, to_apply=%add.1 | all-reduce | flops 16 | bytes 128
  26.6 1.3 gather_fusion
  28.4 14.0 %all-gather.1 = bf16[512,576]{0,1:T(8,128)(2,1)S(1)} all-gather(bf16[128,576]{0,1:T(8,128)(2,1)} %param.19), channel_id=4, replica_groups=mesh['z'=4,'x'=4,'y'=4,'core'=2] {'x'}, dimensions={0}, use_global_device_ids=true | all-gather | bytes 737280 | tf_op jit(solution)/shard_map/all_gather | solution.py:58
  44.1 3.5 %all-to-all-start = ((bf16[4,128,576]{1,2,0:T(8,128)(2,1)}), bf16[4,128,576]{1,2,0:T(8,128)(2,1)S(1)}, u32[]{:S(2)}, u32[]{:S(2)}) async-start(bf16[4,128,576]{1,2,0:T(8,128)(2,1)} %broadcast_select_fusion), calls=%async_computation | async-start | bytes 1179648 | tf_op jit(solution)/shard_map/all_to_all | solution.py:61
  53.4 2.6 all-to-all-done
  57.3 1.5 copy.65
  59.6 1.8 reduce-window.19
  63.0 2.2 convert_bitcast_fusion
  65.1 19.0 %all-gather.4.cloned.1.call-done = bf16[1024,1152]{0,1:T(8,128)(2,1)} async-done(((bf16[128,1152]{0,1:T(8,128)(2,1)}), bf16[1024,1152]{0,1:T(8,128)(2,1)}) %all-gather.4.cloned.1.call-update) | async-done | bytes 2359312 | tf_op jit(solution)/shard_map/all_gather | solution.py:64
  84.1 3.2 %fusion.72 = (bf16[1024,576]{0,1:T(8,128)(2,1)}, bf16[1024,576]{0,1:T(8,128)(2,1)}) fusion(bf16[1024,1152]{0,1:T(8,128)(2,1)} %all-gather.4.cloned.1.call-done), kind=kLoop, calls=%fused_computation.91 | loop fusion | bytes 4718592 | tf_op jit(solution)/shard_map/slice | solution.py:65
  87.4 15.6 %fusion.73 = (f32[128,16]{0,1:T(8,128)S(1)}, bf16[128,16,2048]{2,0,1:T(8,128)(2,1)}) fusion(pred[128,2048]{1,0:T(8,128)(4,1)S(1)} %concatenate.12, bf16[128,16,64]{0,2,1:T(8,128)(2,1)S(1)} %copy-done.6, bf16[128,16,512]{0,2,1:T(8,128)(2,1)S(1)} %copy-done.5, bf16[1024,576]{0,1:T(8,128)(2,1)} %get-tuple-element.5, bf16[1024,576]{0,1:T(8,128)(2,1)} %get-tuple-element.4), kind=kOutput, calls=%fused_computation.92 | convolution fusion | flops 4866443264 | bytes 13377536 | tf_op jit(solution)/shard_map/sub | solution.py:82
  103.0 9.9 %fusion.42 = bf16[16,128,128]{1,2,0:T(8,128)(2,1)S(1)} fusion(bf16[16,512,128]{2,1,0:T(8,128)(2,1)} %param.21, bf16[128,16,2048]{2,0,1:T(8,128)(2,1)} %get-tuple-element.7, bf16[1024,576]{0,1:T(8,128)(2,1)} %get-tuple-element.4, bf16[1024,576]{0,1:T(8,128)(2,1)} %get-tuple-element.5, f32[128,16]{0,1:T(8,128)S(1)} %get-tuple-element.6), kind=kOutput, calls=%fused_computation.46 | convolution fusion | flops 4569956352 | bytes 13377536 | tf_op jit(solution)/shard_map/thc,hcv->thv/dot_general | solution.py:91
  112.9 4.8 %multiply_reduce_fusion = (f32[128]{0:T(128)S(1)}, bf16[128,2048]{1,0:T(8,128)(2,1)S(1)}) fusion(bf16[128,2048]{1,0:T(8,128)(2,1)S(1)} %copy-done.3, bf16[128,2048]{0,1:T(8,128)(2,1)S(1)} %bitcast.103, bf16[2048,2048]{1,0:T(8,128)(2,1)} %param.22), kind=kOutput, calls=%fused_computation.48 | convolution fusion | flops 1075314560 | bytes 9961984 | tf_op jit(solution)/shard_map/dot_general | solution.py:95
  117.7 3.3 %convolution_convert_fusion = bf16[1024,2048]{1,0:T(8,128)(2,1)} fusion(bf16[128,1024]{1,0:T(8,128)(2,1)S(1)} %fusion.30, bf16[128,2048]{1,0:T(8,128)(2,1)S(1)} %get-tuple-element.9, bf16[128,2048]{1,0:T(8,128)(2,1)S(1)} %copy-done.3, f32[2048]{0:T(1024)S(1)} %copy-done.9, f32[128]{0:T(128)S(1)} %add_rsqrt_fusion), kind=kOutput, calls=%fused_computation.14 | convolution fusion | flops 540540928 | bytes 5513728 | tf_op jit(solution)/shard_map/dot_general | solution.py:111
  120.9 10.3 %all-to-all-start.1 = ((bf16[64,16,2048]{2,1,0:T(8,128)(2,1)}), bf16[64,16,2048]{2,1,0:T(8,128)(2,1)}, u32[]{:S(2)}, u32[]{:S(2)}) async-start(bf16[64,16,2048]{2,1,0:T(8,128)(2,1)} %bitcast.99), calls=%async_computation.1 | async-start | bytes 8388608 | tf_op jit(solution)/shard_map/all_to_all | solution.py:118
  131.9 52.9 %all-to-all-done.1 = bf16[64,16,2048]{2,1,0:T(8,128)(2,1)} async-done(((bf16[64,16,2048]{2,1,0:T(8,128)(2,1)}), bf16[64,16,2048]{2,1,0:T(8,128)(2,1)}, u32[]{:S(2)}, u32[]{:S(2)}) %all-to-all-start.1) | async-done | bytes 4194336 | tf_op jit(solution)/shard_map/all_to_all | solution.py:118
  184.8 7.8 %fusion.17 = f32[1024,704]{0,1:T(8,128)} fusion(bf16[1024,2048]{1,0:T(8,128)(2,1)} %bitcast.17, bf16[1,2048,704]{1,2,0:T(8,128)(2,1)} %param.25), kind=kOutput, calls=%fused_computation.25 | convolution fusion | flops 2952790016 | bytes 9961472 | tf_op jit(solution)/shard_map/dot_general | solution.py:122
  192.7 7.8 %fusion.11 = f32[1024,704]{0,1:T(8,128)} fusion(bf16[1024,2048]{1,0:T(8,128)(2,1)} %bitcast.17, bf16[1,2048,704]{1,2,0:T(8,128)(2,1)} %collective-permute-done.1), kind=kOutput, calls=%fused_computation.19 | convolution fusion | flops 2952790016 | bytes 9961472 | tf_op jit(solution)/shard_map/dot_general | solution.py:122
  200.5 12.2 %fusion.15 = bf16[1024,2048]{1,0:T(8,128)(2,1)} fusion(bf16[1,704,2048]{2,1,0:T(8,128)(2,1)} %param.26, f32[1024,704]{0,1:T(8,128)} %fusion.17, bf16[1024,2048]{1,0:T(8,128)(2,1)} %bitcast.17, bf16[1,2048,704]{1,2,0:T(8,128)(2,1)} %param.24), kind=kOutput, calls=%fused_computation.23 | convolution fusion | flops 5909905408 | bytes 17039360 | tf_op jit(solution)/shard_map/dot_general | solution.py:124
  212.7 13.2 %add_convert_fusion = bf16[1024,2048]{1,0:T(8,128)(2,1)} fusion(bf16[1024,2048]{1,0:T(8,128)(2,1)} %fusion.15, bf16[1,704,2048]{2,1,0:T(8,128)(2,1)} %collective-permute-done.2, f32[1024,704]{0,1:T(8,128)} %fusion.11, bf16[1024,2048]{1,0:T(8,128)(2,1)} %bitcast.17, bf16[1,2048,704]{1,2,0:T(8,128)(2,1)} %collective-permute-done), kind=kOutput, calls=%fused_computation.6 | convolution fusion | flops 5920391168 | bytes 21233664 | tf_op jit(solution)/shard_map/dot_general | solution.py:124
  225.9 8.0 %all-to-all-start.2 = ((bf16[64,16,2048]{2,1,0:T(8,128)(2,1)}), bf16[64,16,2048]{2,1,0:T(8,128)(2,1)}, u32[]{:S(2)}, u32[]{:S(2)}) async-start(bf16[64,16,2048]{2,1,0:T(8,128)(2,1)} %bitcast.100), calls=%async_computation.2 | async-start | bytes 8388608 | tf_op jit(solution)/shard_map/all_to_all | solution.py:131
  235.1 52.7 %all-to-all-done.2 = bf16[64,16,2048]{2,1,0:T(8,128)(2,1)} async-done(((bf16[64,16,2048]{2,1,0:T(8,128)(2,1)}), bf16[64,16,2048]{2,1,0:T(8,128)(2,1)}, u32[]{:S(2)}, u32[]{:S(2)}) %all-to-all-start.2) | async-done | bytes 4194336 | tf_op jit(solution)/shard_map/all_to_all | solution.py:131
  287.8 5.1 %fusion.21 = bf16[128,2048]{1,0:T(8,128)(2,1)} fusion(f32[128,1024]{1,0:T(8,128)} %select_reduce_fusion, bf16[1024,2048]{1,0:T(8,128)(2,1)} %bitcast.25, bf16[128,2048]{1,0:T(8,128)(2,1)S(1)} %get-tuple-element.9, bf16[128,2048]{1,0:T(8,128)(2,1)S(1)} %copy-done.3), kind=kOutput, calls=%fused_computation.36 | convolution fusion | flops 3222536192 | bytes 6291456 | tf_op jit(solution)/shard_map/dot_general | solution.py:135
  (67 shorter events, 9.5 us)
Async XLA Ops:
  7.2 55.8 %copy-start = (bf16[16,128,512]{2,1,0:T(8,128)(2,1)S(1)}, bf16[16,128,512]{2,1,0:T(8,128)(2,1)}, u32[]{:S(2)}) copy-start(bf16[16,128,512]{2,1,0:T(8,128)(2,1)} %param.20) | copy-start | bytes 6291460
  27.9 22.2 %copy-start.2 = (s32[16]{0:T(128)S(1)}, s32[16]{0:T(128)}, u32[]{:S(2)}) copy-start(s32[16]{0:T(128)} %param.29) | copy-start | bytes 196
  28.3 27.6 %copy-start.7 = (bf16[128,576]{0,1:T(8,128)(2,1)S(1)}, bf16[128,576]{0,1:T(8,128)(2,1)}, u32[]{:S(2)}) copy-start(bf16[128,576]{0,1:T(8,128)(2,1)} %param.18) | copy-start | bytes 442372
  42.4 14.4 %copy-start.8 = (s32[128,6]{0,1:T(8,128)S(1)}, s32[128,6]{0,1:T(8,128)}, u32[]{:S(2)}) copy-start(s32[128,6]{0,1:T(8,128)} %param.30) | copy-start | bytes 9220
  42.4 14.8 %copy-start.11 = (s32[1,4]{1,0:T(1,128)S(1)}, s32[1,4]{1,0:T(1,128)}, u32[]{:S(2)}) copy-start(s32[1,4]{1,0:T(1,128)} %param.27) | copy-start | bytes 52
  44.1 11.9 %all-to-all-start = ((bf16[4,128,576]{1,2,0:T(8,128)(2,1)}), bf16[4,128,576]{1,2,0:T(8,128)(2,1)S(1)}, u32[]{:S(2)}, u32[]{:S(2)}) async-start(bf16[4,128,576]{1,2,0:T(8,128)(2,1)} %broadcast_select_fusion), calls=%async_computation | async-start | bytes 1179648 | tf_op jit(solution)/shard_map/all_to_all | solution.py:61
  47.6 36.6 %all-gather.4.cloned.1.call-start = ((), (), s32[]{:S(2)}) async-start(), calls=%async_computation.3 | async-start | bytes 2654208 | tf_op jit(solution)/shard_map/all_gather | solution.py:64
  65.1 22.2 %copy-start.5 = (bf16[128,16,512]{0,2,1:T(8,128)(2,1)S(1)}, bf16[128,16,512]{0,2,1:T(8,128)(2,1)}, u32[]{:S(2)}) copy-start(bf16[128,16,512]{0,2,1:T(8,128)(2,1)} %convert_bitcast_fusion) | copy-start | bytes 6291460
  65.1 22.2 %copy-start.6 = (bf16[128,16,64]{0,2,1:T(8,128)(2,1)S(1)}, bf16[128,16,64]{0,2,1:T(8,128)(2,1)}, u32[]{:S(2)}) copy-start(bf16[128,16,64]{0,2,1:T(8,128)(2,1)} %slice.33) | copy-start | bytes 786436
  103.0 9.9 %copy-start.3 = (bf16[128,2048]{1,0:T(8,128)(2,1)S(1)}, bf16[128,2048]{1,0:T(8,128)(2,1)}, u32[]{:S(2)}) copy-start(bf16[128,2048]{1,0:T(8,128)(2,1)} %param.16) | copy-start | bytes 1572868
  112.9 4.8 %copy-start.9 = (f32[2048]{0:T(1024)S(1)}, f32[2048]{0:T(1024)}, u32[]{:S(2)}) copy-start(f32[2048]{0:T(1024)} %param.23) | copy-start | bytes 24580
  117.7 170.1 %copy-start.4 = (bf16[128,2048]{1,0:T(8,128)(2,1)}, bf16[128,2048]{1,0:T(8,128)(2,1)S(1)}, u32[]{:S(2)}) copy-start(bf16[128,2048]{1,0:T(8,128)(2,1)S(1)} %get-tuple-element.9) | copy-start | bytes 1572868
  120.9 63.9 %all-to-all-start.1 = ((bf16[64,16,2048]{2,1,0:T(8,128)(2,1)}), bf16[64,16,2048]{2,1,0:T(8,128)(2,1)}, u32[]{:S(2)}, u32[]{:S(2)}) async-start(bf16[64,16,2048]{2,1,0:T(8,128)(2,1)} %bitcast.99), calls=%async_computation.1 | async-start | bytes 8388608 | tf_op jit(solution)/shard_map/all_to_all | solution.py:118
  131.2 61.5 %collective-permute-start.1 = (bf16[1,2048,704]{1,2,0:T(8,128)(2,1)}, bf16[1,2048,704]{1,2,0:T(8,128)(2,1)}, u32[]{:S(2)}, u32[]{:S(2)}) collective-permute-start(bf16[1,2048,704]{1,2,0:T(8,128)(2,1)} %param.25), channel_id=1, source_target_pairs={{0,1},{1,0},{2,3},{3,2},{4,5},{5,4},{6,7},{7,6},{8,9},{9,8},{10,11... | collective-permute-start | bytes 8650760 | tf_op jit(solution)/shard_map/ppermute | solution.py:116
  131.3 81.3 %collective-permute-start = (bf16[1,2048,704]{1,2,0:T(8,128)(2,1)}, bf16[1,2048,704]{1,2,0:T(8,128)(2,1)}, u32[]{:S(2)}, u32[]{:S(2)}) collective-permute-start(bf16[1,2048,704]{1,2,0:T(8,128)(2,1)} %param.24), channel_id=1, source_target_pairs={{0,1},{1,0},{2,3},{3,2},{4,5},{5,4},{6,7},{7,6},{8,9},{9,8},{10,11... | collective-permute-start | bytes 8650760 | tf_op jit(solution)/shard_map/ppermute | solution.py:115
  131.8 80.8 %collective-permute-start.2 = (bf16[1,704,2048]{2,1,0:T(8,128)(2,1)}, bf16[1,704,2048]{2,1,0:T(8,128)(2,1)}, u32[]{:S(2)}, u32[]{:S(2)}) collective-permute-start(bf16[1,704,2048]{2,1,0:T(8,128)(2,1)} %param.26), channel_id=1, source_target_pairs={{0,1},{1,0},{2,3},{3,2},{4,5},{5,4},{6,7},{7,6},{8,9},{9,8},{10,11... | collective-permute-start | bytes 8650760 | tf_op jit(solution)/shard_map/ppermute | solution.py:117
  225.9 8.0 %copy-start.10 = (f32[128,6]{0,1:T(8,128)S(1)}, f32[128,6]{0,1:T(8,128)}, u32[]{:S(2)}) copy-start(f32[128,6]{0,1:T(8,128)} %param.31) | copy-start | bytes 9220
  225.9 61.9 %all-to-all-start.2 = ((bf16[64,16,2048]{2,1,0:T(8,128)(2,1)}), bf16[64,16,2048]{2,1,0:T(8,128)(2,1)}, u32[]{:S(2)}, u32[]{:S(2)}) async-start(bf16[64,16,2048]{2,1,0:T(8,128)(2,1)} %bitcast.100), calls=%async_computation.2 | async-start | bytes 8388608 | tf_op jit(solution)/shard_map/all_to_all | solution.py:131
  287.8 5.2 %copy-start.1 = (bf16[16,128,512]{2,1,0:T(8,128)(2,1)S(1)}, bf16[16,128,512]{2,1,0:T(8,128)(2,1)}, u32[]{:S(2)}) copy-start(bf16[16,128,512]{2,1,0:T(8,128)(2,1)} %param.20) | copy-start | bytes 6291460
Sparse Core Ops, SparseCore 0:
  56.9 27.2 all-gather.3

commit v3 on v2

--- a/solution.py
+++ b/solution.py
@@ -37,33 +37,26 @@
     head_count = uk_weight.shape[0]
     nope_width = uk_weight.shape[1]
     kv_rank = uk_weight.shape[2]
-    latent_width = suffix_latent.shape[1]
     rope_width = queries.shape[1] // head_count - nope_width
     score_scale = (nope_width + rope_width) ** (-0.5)
     column = lax.axis_index("y") * lax.axis_size("core") + lax.axis_index("core")
     positions = column * tok_rows + jnp.arange(tok_rows, dtype=jnp.int32)
     lengths = suffix_lengths[0]
     own_request = request_of(positions, lengths)
-    my_group = lax.axis_index("z") * lax.axis_size("x") + lax.axis_index("x")
-    my_slot = prefix_owner[prefix_ids[my_group, 0]]
+    my_slot = prefix_owner[prefix_ids[0, 0]]
     q_split = queries.reshape(tok_rows, head_count, nope_width + rope_width)
     q_latent = jnp.einsum(
         "thn,hnc->thc", q_split[:, :, :nope_width], uk_weight, preferred_element_type=jnp.float32
     ).astype(jnp.bfloat16)
     q_abs = jnp.concatenate([q_latent, q_split[:, :, nope_width:]], axis=2)
     x_count = lax.axis_size("x")
-    z_count = lax.axis_size("z")
-    my_x = lax.axis_index("x")
-    group_slots = prefix_owner[prefix_ids[:, 0]]
+    suffix_rows = lax.all_gather(suffix_latent, ("y", "core"), axis=0, tiled=True)
+    dest_slots = lax.all_gather(my_slot[None], "z", axis=0, tiled=True)
     x_chunks = lax.all_gather(prefix_latent, "x", axis=0, tiled=False)
-    dest_slots = group_slots.reshape(z_count, x_count)[:, my_x]
     sent = jnp.take(x_chunks, dest_slots % x_count, axis=0)
     recv_chunks = lax.all_to_all(sent, "z", 0, 0, tiled=True)
     my_chunk = lax.dynamic_index_in_dim(recv_chunks, my_slot // x_count, 0, keepdims=False)
-    both = jnp.concatenate([my_chunk, suffix_latent], axis=1)
-    gathered = lax.all_gather(both, ("y", "core"), axis=0, tiled=True)
-    prefix_rows = gathered[:, :latent_width]
-    suffix_rows = gathered[:, latent_width:]
+    prefix_rows = lax.all_gather(my_chunk, ("y", "core"), axis=0, tiled=True)
     key_rows = jnp.concatenate([prefix_rows, suffix_rows], axis=0)
     key_pos = jnp.arange(suffix_rows.shape[0], dtype=jnp.int32)
     key_request = request_of(key_pos, lengths)
@@ -165,7 +158,7 @@
         P(rows, None, None),
         P(rows, None, None),
         P(groups, None),
-        P(),
+        P(groups, None),
         P(),
         P(rows, None),
         P(rows, None),

time: 300 us -> 287 us (0.957)
  blocking collectives: 30.7 us -> 23.7 us
  local copies, waits for them, and re-layouts: 11.7 us -> 8.49 us
    unnamed x1, blocking collectives: 16.7 us -> 9.73 us
    all_gather x1 -> x2, waiting for transfers between devices: 19 us -> 15.1 us  [the longest x1 15.1 us: layer(): prefix_rows = lax.all_gather(my_chunk, ('y', 'core'), axis=0, tiled=True)]
    slice x2 -> x1, local copies, waits for them, and re-layouts: 3.52 us -> 0.28 us  [the longest x1 3.24 us: layer(): prefix_rows = gathered[:, :latent_width]]
    all_to_all x1, waiting for transfers between devices: 2.6 us -> 5.74 us  [layer(): recv_chunks = lax.all_to_all(sent, 'z', 0, 0, tiled=True)]
  transfers between devices with their start and end apart: 7 -> 8, of which waited for: 4 -> 4; matrix products, arithmetic and copies ran while one was open for 13% -> 15% of each run, Pallas kernels for 0% -> 0%
where the time goes in v3:
time: 287 us; the launch traced here: 286 us
  waiting for transfers between devices  127 us (44%)
  matrix products  82 us (29%)
  blocking collectives  23.7 us (8%)
  starting transfers between devices  22.3 us (8%)
  between operations  17.5 us (6%)
  local copies, waits for them, and re-layouts  8.49 us (3%)
  other arithmetic  5.21 us (2%)
    all_to_all x1, waiting for transfers between devices, layer(): recv_rows = lax.all_to_all(packed, ('z', 'x', 'y'), 0, 0, tiled=True)  53 us
    all_to_all x1, waiting for transfers between devices, layer(): returned = lax.all_to_all(pair_total, ('z', 'x', 'y'), 0, 0, tiled=True)  52.7 us
    dot_general x2, matrix products, half_expert(): jnp.dot(active, down_w, preferred_element_type=jnp.float32)  25.4 us
    sub x1, matrix products, layer(): scores - top_score  16.1 us
    dot_general x2, matrix products, half_expert(): up_proj = jnp.dot(recv_rows, up_w, preferred_element_type=jnp.float32)  15.6 us
    all_gather x1, waiting for transfers between devices, layer(): prefix_rows = lax.all_gather(my_chunk, ('y', 'core'), axis=0, tiled=True)  15.1 us
    all_gather x1, blocking collectives, layer(): x_chunks = lax.all_gather(prefix_latent, 'x', axis=0, tiled=False)  14 us
    all_to_all x1, starting transfers between devices, layer(): recv_rows = lax.all_to_all(packed, ('z', 'x', 'y'), 0, 0, tiled=True)  10.2 us
  transfers between devices with their start and end apart: 8, of which 4 were waited for; matrix products, arithmetic and copies ran while one was open for 15% of the time, Pallas kernels for 0%

profile of v3, /device:TPU:2, one launch (start us, length us, event | category | flops | bytes accessed | tf_op | source)
XLA Modules:
  0.0 286.4 jit_solution(6141998200900885450)
XLA Ops:
  8.6 1.2 dynamic_slice.7
  9.8 1.2 dynamic-slice
  11.1 1.4 dynamic-update-slice
  12.5 9.7 %all-reduce.1 = s32[4]{0:T(128)S(1)} all-reduce(s32[4]{0:T(128)S(1)} %dynamic-update-slice), channel_id=1, replica_groups=mesh['z'=4,'x'=4,'y'=4,'core'=2] {'z'}, use_global_device_ids=true, to_apply=%add.1 | all-reduce | flops 4 | bytes 32
  22.2 14.0 %all-gather = bf16[512,576]{0,1:T(8,128)(2,1)S(1)} all-gather(bf16[128,576]{0,1:T(8,128)(2,1)} %param.19), channel_id=2, replica_groups=mesh['z'=4,'x'=4,'y'=4,'core'=2] {'x'}, dimensions={0}, use_global_device_ids=true | all-gather | bytes 737280 | tf_op jit(solution)/shard_map/all_gather | solution.py:55
  38.0 3.5 %all-to-all-start = ((bf16[4,128,576]{1,2,0:T(8,128)(2,1)}), bf16[4,128,576]{1,2,0:T(8,128)(2,1)S(1)}, u32[]{:S(2)}, u32[]{:S(2)}) async-start(bf16[4,128,576]{1,2,0:T(8,128)(2,1)} %broadcast_select_fusion), calls=%async_computation | async-start | bytes 1179648 | tf_op jit(solution)/shard_map/all_to_all | solution.py:57
  44.1 5.7 %all-to-all-done = bf16[4,128,576]{1,2,0:T(8,128)(2,1)S(1)} async-done(((bf16[4,128,576]{1,2,0:T(8,128)(2,1)}), bf16[4,128,576]{1,2,0:T(8,128)(2,1)S(1)}, u32[]{:S(2)}, u32[]{:S(2)}) %all-to-all-start) | async-done | bytes 589856 | tf_op jit(solution)/shard_map/all_to_all | solution.py:57
  51.1 1.5 copy.65
  53.4 1.8 reduce-window.19
  56.8 2.1 convert_bitcast_fusion
  58.9 15.1 %all-gather.7.cloned.1.call-done = bf16[1,1024,576]{1,2,0:T(8,128)(2,1)} async-done(((bf16[1,128,576]{1,2,0:T(8,128)(2,1)}), bf16[1,1024,576]{1,2,0:T(8,128)(2,1)}) %all-gather.7.cloned.1.call-update) | async-done | bytes 1179664 | tf_op jit(solution)/shard_map/all_gather | solution.py:59
  73.9 16.1 %fusion.71 = (f32[128,16]{0,1:T(8,128)S(1)}, bf16[128,16,2048]{2,0,1:T(8,128)(2,1)}) fusion(pred[128,2048]{1,0:T(8,128)(4,1)S(1)} %concatenate.9, bf16[128,16,64]{0,2,1:T(8,128)(2,1)} %slice.23, bf16[128,16,512]{0,2,1:T(8,128)(2,1)} %convert_bitcast_fusion, bf16[1024,576]{0,1:T(8,128)(2,1)} %all-gather.5.cloned.1.call-done, bf16[1024,576]{0,1:T(8,128)(2,1)} %bitcast.103), kind=kOutput, calls=%fused_computation.85 | convolution fusion | flops 4866443264 | bytes 13377536 | tf_op jit(solution)/shard_map/sub | solution.py:75
  90.0 9.6 %fusion.42 = bf16[16,128,128]{1,2,0:T(8,128)(2,1)S(1)} fusion(bf16[16,512,128]{2,1,0:T(8,128)(2,1)} %param.21, bf16[128,16,2048]{2,0,1:T(8,128)(2,1)} %get-tuple-element.5, bf16[1024,576]{0,1:T(8,128)(2,1)} %bitcast.104, bf16[1024,576]{0,1:T(8,128)(2,1)S(1)} %copy-done.7, f32[128,16]{0,1:T(8,128)S(1)} %get-tuple-element.4), kind=kOutput, calls=%fused_computation.45 | convolution fusion | flops 4569956352 | bytes 13377536 | tf_op jit(solution)/shard_map/thc,hcv->thv/dot_general | solution.py:84
  99.7 4.8 %multiply_reduce_fusion = (f32[128]{0:T(128)S(1)}, bf16[128,2048]{1,0:T(8,128)(2,1)S(1)}) fusion(bf16[128,2048]{1,0:T(8,128)(2,1)S(1)} %copy-done.2, bf16[128,2048]{0,1:T(8,128)(2,1)S(1)} %bitcast.99, bf16[2048,2048]{1,0:T(8,128)(2,1)} %param.22), kind=kOutput, calls=%fused_computation.47 | convolution fusion | flops 1075314560 | bytes 9961984 | tf_op jit(solution)/shard_map/dot_general | solution.py:88
  104.5 3.3 %convolution_convert_fusion = bf16[1024,2048]{1,0:T(8,128)(2,1)} fusion(bf16[128,1024]{1,0:T(8,128)(2,1)S(1)} %fusion.30, bf16[128,2048]{1,0:T(8,128)(2,1)S(1)} %get-tuple-element.7, bf16[128,2048]{1,0:T(8,128)(2,1)S(1)} %copy-done.2, f32[2048]{0:T(1024)S(1)} %copy-done.5, f32[128]{0:T(128)S(1)} %add_rsqrt_fusion), kind=kOutput, calls=%fused_computation.13 | convolution fusion | flops 540540928 | bytes 5513728 | tf_op jit(solution)/shard_map/dot_general | solution.py:104
  107.7 10.2 %all-to-all-start.1 = ((bf16[64,16,2048]{2,1,0:T(8,128)(2,1)}), bf16[64,16,2048]{2,1,0:T(8,128)(2,1)}, u32[]{:S(2)}, u32[]{:S(2)}) async-start(bf16[64,16,2048]{2,1,0:T(8,128)(2,1)} %bitcast.95), calls=%async_computation.1 | async-start | bytes 8388608 | tf_op jit(solution)/shard_map/all_to_all | solution.py:111
  118.7 53.0 %all-to-all-done.1 = bf16[64,16,2048]{2,1,0:T(8,128)(2,1)} async-done(((bf16[64,16,2048]{2,1,0:T(8,128)(2,1)}), bf16[64,16,2048]{2,1,0:T(8,128)(2,1)}, u32[]{:S(2)}, u32[]{:S(2)}) %all-to-all-start.1) | async-done | bytes 4194336 | tf_op jit(solution)/shard_map/all_to_all | solution.py:111
  171.6 7.9 %fusion.17 = f32[1024,704]{0,1:T(8,128)} fusion(bf16[1024,2048]{1,0:T(8,128)(2,1)} %bitcast.14, bf16[1,2048,704]{1,2,0:T(8,128)(2,1)} %param.25), kind=kOutput, calls=%fused_computation.24 | convolution fusion | flops 2952790016 | bytes 9961472 | tf_op jit(solution)/shard_map/dot_general | solution.py:115
  179.5 7.8 %fusion.11 = f32[1024,704]{0,1:T(8,128)} fusion(bf16[1024,2048]{1,0:T(8,128)(2,1)} %bitcast.14, bf16[1,2048,704]{1,2,0:T(8,128)(2,1)} %collective-permute-done.1), kind=kOutput, calls=%fused_computation.18 | convolution fusion | flops 2952790016 | bytes 9961472 | tf_op jit(solution)/shard_map/dot_general | solution.py:115
  187.3 12.2 %fusion.15 = bf16[1024,2048]{1,0:T(8,128)(2,1)} fusion(bf16[1,704,2048]{2,1,0:T(8,128)(2,1)} %param.26, f32[1024,704]{0,1:T(8,128)} %fusion.17, bf16[1024,2048]{1,0:T(8,128)(2,1)} %bitcast.14, bf16[1,2048,704]{1,2,0:T(8,128)(2,1)} %param.24), kind=kOutput, calls=%fused_computation.22 | convolution fusion | flops 5909905408 | bytes 17039360 | tf_op jit(solution)/shard_map/dot_general | solution.py:117
  199.5 13.2 %add_convert_fusion = bf16[1024,2048]{1,0:T(8,128)(2,1)} fusion(bf16[1024,2048]{1,0:T(8,128)(2,1)} %fusion.15, bf16[1,704,2048]{2,1,0:T(8,128)(2,1)} %collective-permute-done.2, f32[1024,704]{0,1:T(8,128)} %fusion.11, bf16[1024,2048]{1,0:T(8,128)(2,1)} %bitcast.14, bf16[1,2048,704]{1,2,0:T(8,128)(2,1)} %collective-permute-done), kind=kOutput, calls=%fused_computation.5 | convolution fusion | flops 5920391168 | bytes 21233664 | tf_op jit(solution)/shard_map/dot_general | solution.py:117
  212.7 7.8 %all-to-all-start.2 = ((bf16[64,16,2048]{2,1,0:T(8,128)(2,1)}), bf16[64,16,2048]{2,1,0:T(8,128)(2,1)}, u32[]{:S(2)}, u32[]{:S(2)}) async-start(bf16[64,16,2048]{2,1,0:T(8,128)(2,1)} %bitcast.96), calls=%async_computation.2 | async-start | bytes 8388608 | tf_op jit(solution)/shard_map/all_to_all | solution.py:124
  221.7 52.7 %all-to-all-done.2 = bf16[64,16,2048]{2,1,0:T(8,128)(2,1)} async-done(((bf16[64,16,2048]{2,1,0:T(8,128)(2,1)}), bf16[64,16,2048]{2,1,0:T(8,128)(2,1)}, u32[]{:S(2)}, u32[]{:S(2)}) %all-to-all-start.2) | async-done | bytes 4194336 | tf_op jit(solution)/shard_map/all_to_all | solution.py:124
  274.4 5.1 %fusion.21 = bf16[128,2048]{1,0:T(8,128)(2,1)} fusion(f32[128,1024]{1,0:T(8,128)} %select_reduce_fusion, bf16[1024,2048]{1,0:T(8,128)(2,1)} %bitcast.22, bf16[128,2048]{1,0:T(8,128)(2,1)S(1)} %get-tuple-element.7, bf16[128,2048]{1,0:T(8,128)(2,1)S(1)} %copy-done.2), kind=kOutput, calls=%fused_computation.35 | convolution fusion | flops 3222536192 | bytes 6291456 | tf_op jit(solution)/shard_map/dot_general | solution.py:128
  (56 shorter events, 8.0 us)
Async XLA Ops:
  7.2 49.6 %copy-start = (bf16[16,128,512]{2,1,0:T(8,128)(2,1)S(1)}, bf16[16,128,512]{2,1,0:T(8,128)(2,1)}, u32[]{:S(2)}) copy-start(bf16[16,128,512]{2,1,0:T(8,128)(2,1)} %param.20) | copy-start | bytes 6291460
  7.2 51.7 %all-gather.5.cloned.1.call-start = ((), (), s32[]{:S(2)}) async-start(), calls=%async_computation.3 | async-start | bytes 1327104 | tf_op jit(solution)/shard_map/all_gather | solution.py:53
  22.2 28.3 %copy-start.4 = (s32[128,6]{0,1:T(8,128)S(1)}, s32[128,6]{0,1:T(8,128)}, u32[]{:S(2)}) copy-start(s32[128,6]{0,1:T(8,128)} %param.30) | copy-start | bytes 9220
  36.2 14.7 %copy-start.8 = (s32[1,4]{1,0:T(1,128)S(1)}, s32[1,4]{1,0:T(1,128)}, u32[]{:S(2)}) copy-start(s32[1,4]{1,0:T(1,128)} %param.27) | copy-start | bytes 52
  38.0 11.9 %all-to-all-start = ((bf16[4,128,576]{1,2,0:T(8,128)(2,1)}), bf16[4,128,576]{1,2,0:T(8,128)(2,1)S(1)}, u32[]{:S(2)}, u32[]{:S(2)}) async-start(bf16[4,128,576]{1,2,0:T(8,128)(2,1)} %broadcast_select_fusion), calls=%async_computation | async-start | bytes 1179648 | tf_op jit(solution)/shard_map/all_to_all | solution.py:57
  41.4 32.5 %all-gather.7.cloned.1.call-start = ((), (), s32[]{:S(2)}) async-start(), calls=%async_computation.4 | async-start | bytes 1327104 | tf_op jit(solution)/shard_map/all_gather | solution.py:59
  73.9 16.1 %copy-start.7 = (bf16[1024,576]{0,1:T(8,128)(2,1)S(1)}, bf16[1024,576]{0,1:T(8,128)(2,1)}, u32[]{:S(2)}) copy-start(bf16[1024,576]{0,1:T(8,128)(2,1)} %all-gather.5.cloned.1.call-done) | copy-start | bytes 3538948
  90.0 9.6 %copy-start.2 = (bf16[128,2048]{1,0:T(8,128)(2,1)S(1)}, bf16[128,2048]{1,0:T(8,128)(2,1)}, u32[]{:S(2)}) copy-start(bf16[128,2048]{1,0:T(8,128)(2,1)} %param.16) | copy-start | bytes 1572868
  99.7 4.8 %copy-start.5 = (f32[2048]{0:T(1024)S(1)}, f32[2048]{0:T(1024)}, u32[]{:S(2)}) copy-start(f32[2048]{0:T(1024)} %param.23) | copy-start | bytes 24580
  104.4 170.0 %copy-start.3 = (bf16[128,2048]{1,0:T(8,128)(2,1)}, bf16[128,2048]{1,0:T(8,128)(2,1)S(1)}, u32[]{:S(2)}) copy-start(bf16[128,2048]{1,0:T(8,128)(2,1)S(1)} %get-tuple-element.7) | copy-start | bytes 1572868
  107.7 63.9 %all-to-all-start.1 = ((bf16[64,16,2048]{2,1,0:T(8,128)(2,1)}), bf16[64,16,2048]{2,1,0:T(8,128)(2,1)}, u32[]{:S(2)}, u32[]{:S(2)}) async-start(bf16[64,16,2048]{2,1,0:T(8,128)(2,1)} %bitcast.95), calls=%async_computation.1 | async-start | bytes 8388608 | tf_op jit(solution)/shard_map/all_to_all | solution.py:111
  118.0 61.5 %collective-permute-start.1 = (bf16[1,2048,704]{1,2,0:T(8,128)(2,1)}, bf16[1,2048,704]{1,2,0:T(8,128)(2,1)}, u32[]{:S(2)}, u32[]{:S(2)}) collective-permute-start(bf16[1,2048,704]{1,2,0:T(8,128)(2,1)} %param.25), channel_id=1, source_target_pairs={{0,1},{1,0},{2,3},{3,2},{4,5},{5,4},{6,7},{7,6},{8,9},{9,8},{10,11... | collective-permute-start | bytes 8650760 | tf_op jit(solution)/shard_map/ppermute | solution.py:109
  118.1 81.4 %collective-permute-start = (bf16[1,2048,704]{1,2,0:T(8,128)(2,1)}, bf16[1,2048,704]{1,2,0:T(8,128)(2,1)}, u32[]{:S(2)}, u32[]{:S(2)}) collective-permute-start(bf16[1,2048,704]{1,2,0:T(8,128)(2,1)} %param.24), channel_id=1, source_target_pairs={{0,1},{1,0},{2,3},{3,2},{4,5},{5,4},{6,7},{7,6},{8,9},{9,8},{10,11... | collective-permute-start | bytes 8650760 | tf_op jit(solution)/shard_map/ppermute | solution.py:108
  118.6 80.9 %collective-permute-start.2 = (bf16[1,704,2048]{2,1,0:T(8,128)(2,1)}, bf16[1,704,2048]{2,1,0:T(8,128)(2,1)}, u32[]{:S(2)}, u32[]{:S(2)}) collective-permute-start(bf16[1,704,2048]{2,1,0:T(8,128)(2,1)} %param.26), channel_id=1, source_target_pairs={{0,1},{1,0},{2,3},{3,2},{4,5},{5,4},{6,7},{7,6},{8,9},{9,8},{10,11... | collective-permute-start | bytes 8650760 | tf_op jit(solution)/shard_map/ppermute | solution.py:110
  212.7 7.8 %copy-start.6 = (f32[128,6]{0,1:T(8,128)S(1)}, f32[128,6]{0,1:T(8,128)}, u32[]{:S(2)}) copy-start(f32[128,6]{0,1:T(8,128)} %param.31) | copy-start | bytes 9220
  212.7 61.7 %all-to-all-start.2 = ((bf16[64,16,2048]{2,1,0:T(8,128)(2,1)}), bf16[64,16,2048]{2,1,0:T(8,128)(2,1)}, u32[]{:S(2)}, u32[]{:S(2)}) async-start(bf16[64,16,2048]{2,1,0:T(8,128)(2,1)} %bitcast.96), calls=%async_computation.2 | async-start | bytes 8388608 | tf_op jit(solution)/shard_map/all_to_all | solution.py:124
  274.4 5.2 %copy-start.1 = (bf16[16,128,512]{2,1,0:T(8,128)(2,1)S(1)}, bf16[16,128,512]{2,1,0:T(8,128)(2,1)}, u32[]{:S(2)}) copy-start(bf16[16,128,512]{2,1,0:T(8,128)(2,1)} %param.20) | copy-start | bytes 6291460
Sparse Core Ops, SparseCore 0:
  9.7 26.0 all-gather.4
  50.6 23.2 all-gather.6

commit v4 on v3

--- a/solution.py
+++ b/solution.py
@@ -50,9 +50,14 @@
     ).astype(jnp.bfloat16)
     q_abs = jnp.concatenate([q_latent, q_split[:, :, nope_width:]], axis=2)
     x_count = lax.axis_size("x")
+    z_count = lax.axis_size("z")
     suffix_rows = lax.all_gather(suffix_latent, ("y", "core"), axis=0, tiled=True)
-    dest_slots = lax.all_gather(my_slot[None], "z", axis=0, tiled=True)
-    x_chunks = lax.all_gather(prefix_latent, "x", axis=0, tiled=False)
+    dest_slots = lax.all_to_all(
+        jnp.broadcast_to(my_slot[None], (z_count,)), "z", 0, 0, tiled=True
+    )
+    x_chunks = lax.all_to_all(
+        jnp.broadcast_to(prefix_latent[None], (x_count,) + prefix_latent.shape), "x", 0, 0, tiled=True
+    )
     sent = jnp.take(x_chunks, dest_slots % x_count, axis=0)
     recv_chunks = lax.all_to_all(sent, "z", 0, 0, tiled=True)
     my_chunk = lax.dynamic_index_in_dim(recv_chunks, my_slot // x_count, 0, keepdims=False)
@@ -113,7 +118,7 @@
     def half_expert(gate_w, up_w, down_w):
         gate_proj = jnp.dot(recv_rows, gate_w, preferred_element_type=jnp.float32)
         up_proj = jnp.dot(recv_rows, up_w, preferred_element_type=jnp.float32)
-        active = (jax.nn.silu(gate_proj) * up_proj).astype(jnp.bfloat16)
+        active = lax.optimization_barrier((jax.nn.silu(gate_proj) * up_proj).astype(jnp.bfloat16))
         return jnp.dot(active, down_w, preferred_element_type=jnp.float32).astype(jnp.bfloat16)
 
     own_part = half_expert(expert_gate[0], expert_up[0], expert_down[0])

time: 287 us -> 278 us (0.969)
  blocking collectives: 23.7 us -> 10.4 us
  matrix products: 82 us -> 75 us
  waiting for transfers between devices: 127 us -> 133 us
  starting transfers between devices: 22.3 us -> 27.4 us
    dot_general x2, matrix products: 25.4 us -> 10.5 us  [half_expert(): jnp.dot(active, down_w, preferred_element_type=jnp.float32)]
    all_gather x1 -> x0, blocking collectives: 14 us -> none  [layer(): x_chunks = lax.all_gather(prefix_latent, 'x', axis=0, tiled=False)]
    dot_general x0 -> x2, matrix products: none -> 11.7 us  [half_expert(): gate_proj = jnp.dot(recv_rows, gate_w, preferred_element_type=jnp.float32)]
    all_to_all x0 -> x1, blocking collectives: none -> 10.4 us  [layer(): lax.all_to_all(jnp.broadcast_to(my_slot[None], (z_count,)), 'z', 0, 0, ti...]
    unnamed x1 -> x0, blocking collectives: 9.73 us -> none
    all_to_all x0 -> x1, waiting for transfers between devices: none -> 7.07 us  [layer(): lax.all_to_all(jnp.broadcast_to(prefix_latent[None], (x_count,) + prefix_...]
    all_to_all x1, waiting for transfers between devices: 53 us -> 47.9 us  [layer(): recv_rows = lax.all_to_all(packed, ('z', 'x', 'y'), 0, 0, tiled=True)]
    ppermute x1, waiting for transfers between devices: 0.01 us -> 5.02 us  [layer(): sibling_gate = lax.ppermute(expert_gate, 'core', swap)]
  transfers between devices with their start and end apart: 8 -> 9, of which waited for: 4 -> 6; matrix products, arithmetic and copies ran while one was open for 15% -> 15% of each run, Pallas kernels for 0% -> 0%
where the time goes in v4:
time: 278 us; the launch traced here: 277 us
  waiting for transfers between devices  133 us (48%)
  matrix products  75 us (27%)
  starting transfers between devices  27.4 us (10%)
  between operations  17.6 us (6%)
  blocking collectives  10.4 us (4%)
  local copies, waits for them, and re-layouts  8.22 us (3%)
  other arithmetic  5.39 us (2%)
    all_to_all x1, waiting for transfers between devices, layer(): returned = lax.all_to_all(pair_total, ('z', 'x', 'y'), 0, 0, tiled=True)  52.7 us
    all_to_all x1, waiting for transfers between devices, layer(): recv_rows = lax.all_to_all(packed, ('z', 'x', 'y'), 0, 0, tiled=True)  47.9 us
    sub x1, matrix products, layer(): scores - top_score  16 us
    all_gather x1, waiting for transfers between devices, layer(): prefix_rows = lax.all_gather(my_chunk, ('y', 'core'), axis=0, tiled=True)  14 us
    dot_general x2, matrix products, half_expert(): up_proj = jnp.dot(recv_rows, up_w, preferred_element_type=jnp.float32)  11.8 us
    dot_general x2, matrix products, half_expert(): gate_proj = jnp.dot(recv_rows, gate_w, preferred_element_type=jnp.float32)  11.7 us
    dot_general x2, matrix products, half_expert(): jnp.dot(active, down_w, preferred_element_type=jnp.float32)  10.5 us
    all_to_all x1, blocking collectives, layer(): lax.all_to_all(jnp.broadcast_to(my_slot[None], (z_count,)), 'z', 0, 0, ti...  10.4 us
  transfers between devices with their start and end apart: 9, of which 6 were waited for; matrix products, arithmetic and copies ran while one was open for 15% of the time, Pallas kernels for 0%

profile of v4, /device:TPU:2, one launch (start us, length us, event | category | flops | bytes accessed | tf_op | source)
XLA Modules:
  0.0 277.3 jit_solution(16806053846315618564)
XLA Ops:
  10.5 10.4 %all_to_all.46 = s32[4,1,1]{2,1,0:T(1,128)S(1)} all-to-all(s32[4,1,1]{2,1,0:T(1,128)S(1)} %broadcast_in_dim.74), channel_id=1, replica_groups=mesh['z'=4,'x'=4,'y'=4,'core'=2] {'z'}, dimensions={0} | all-to-all | bytes 32 | tf_op jit(solution)/shard_map/all_to_all | solution.py:55
  20.9 1.8 broadcast_in_dim.76
  22.7 5.0 %all-to-all-start.1 = ((bf16[4,128,576]{1,2,0:T(8,128)(2,1)}), bf16[4,128,576]{1,2,0:T(8,128)(2,1)S(1)}, u32[]{:S(2)}, u32[]{:S(2)}) async-start(bf16[4,128,576]{1,2,0:T(8,128)(2,1)} %broadcast_in_dim.76), calls=%async_computation.1 | async-start | bytes 1179648 | tf_op jit(solution)/shard_map/all_to_all | solution.py:58
  27.8 7.1 %all-to-all-done.1 = bf16[4,128,576]{1,2,0:T(8,128)(2,1)S(1)} async-done(((bf16[4,128,576]{1,2,0:T(8,128)(2,1)}), bf16[4,128,576]{1,2,0:T(8,128)(2,1)S(1)}, u32[]{:S(2)}, u32[]{:S(2)}) %all-to-all-start.1) | async-done | bytes 589856 | tf_op jit(solution)/shard_map/all_to_all | solution.py:58
  36.5 3.5 %all-to-all-start.2 = ((bf16[4,128,576]{1,2,0:T(8,128)(2,1)}), bf16[4,128,576]{1,2,0:T(8,128)(2,1)S(1)}, u32[]{:S(2)}, u32[]{:S(2)}) async-start(bf16[4,128,576]{1,2,0:T(8,128)(2,1)} %broadcast_select_fusion), calls=%async_computation.2 | async-start | bytes 1179648 | tf_op jit(solution)/shard_map/all_to_all | solution.py:62
  42.6 5.7 %all-to-all-done.2 = bf16[4,128,576]{1,2,0:T(8,128)(2,1)S(1)} async-done(((bf16[4,128,576]{1,2,0:T(8,128)(2,1)}), bf16[4,128,576]{1,2,0:T(8,128)(2,1)S(1)}, u32[]{:S(2)}, u32[]{:S(2)}) %all-to-all-start.2) | async-done | bytes 589856 | tf_op jit(solution)/shard_map/all_to_all | solution.py:62
  55.3 2.2 convert_bitcast_fusion
  57.5 14.0 %all-gather.6.cloned.1.call-done = bf16[1,1024,576]{1,2,0:T(8,128)(2,1)} async-done(((bf16[1,128,576]{1,2,0:T(8,128)(2,1)}), bf16[1,1024,576]{1,2,0:T(8,128)(2,1)}) %all-gather.6.cloned.1.call-update) | async-done | bytes 1179664 | tf_op jit(solution)/shard_map/all_gather | solution.py:64
  71.5 16.0 %fusion.64 = (f32[128,16]{0,1:T(8,128)S(1)}, bf16[128,16,2048]{2,0,1:T(8,128)(2,1)}) fusion(pred[128,2048]{1,0:T(8,128)(4,1)S(1)} %concatenate.9, bf16[128,16,64]{0,2,1:T(8,128)(2,1)} %slice.23, bf16[128,16,512]{0,2,1:T(8,128)(2,1)} %convert_bitcast_fusion, bf16[1024,576]{0,1:T(8,128)(2,1)} %all-gather.4.cloned.1.call-done, bf16[1024,576]{0,1:T(8,128)(2,1)} %bitcast.99), kind=kOutput, calls=%fused_computation.87 | convolution fusion | flops 4866443264 | bytes 13377536 | tf_op jit(solution)/shard_map/sub | solution.py:80
  87.6 9.6 %fusion.41 = bf16[16,128,128]{1,2,0:T(8,128)(2,1)S(1)} fusion(bf16[16,512,128]{2,1,0:T(8,128)(2,1)} %param.21, bf16[128,16,2048]{2,0,1:T(8,128)(2,1)} %get-tuple-element.3, bf16[1024,576]{0,1:T(8,128)(2,1)} %bitcast.100, bf16[1024,576]{0,1:T(8,128)(2,1)S(1)} %copy-done.10, f32[128,16]{0,1:T(8,128)S(1)} %get-tuple-element.2), kind=kOutput, calls=%fused_computation.44 | convolution fusion | flops 4569956352 | bytes 13377536 | tf_op jit(solution)/shard_map/thc,hcv->thv/dot_general | solution.py:89
  97.2 4.8 %multiply_reduce_fusion = (f32[128]{0:T(128)S(1)}, bf16[128,2048]{1,0:T(8,128)(2,1)S(1)}) fusion(bf16[128,2048]{1,0:T(8,128)(2,1)S(1)} %copy-done.2, bf16[128,2048]{0,1:T(8,128)(2,1)S(1)} %bitcast.95, bf16[2048,2048]{1,0:T(8,128)(2,1)} %param.22), kind=kOutput, calls=%fused_computation.46 | convolution fusion | flops 1075314560 | bytes 9961984 | tf_op jit(solution)/shard_map/dot_general | solution.py:93
  102.0 3.3 %convolution_convert_fusion = bf16[1024,2048]{1,0:T(8,128)(2,1)} fusion(bf16[128,1024]{1,0:T(8,128)(2,1)S(1)} %fusion.30, bf16[128,2048]{1,0:T(8,128)(2,1)S(1)} %get-tuple-element.5, bf16[128,2048]{1,0:T(8,128)(2,1)S(1)} %copy-done.2, f32[2048]{0:T(1024)S(1)} %copy-done.5, f32[128]{0:T(128)S(1)} %add_rsqrt_fusion), kind=kOutput, calls=%fused_computation.13 | convolution fusion | flops 540540928 | bytes 5513728 | tf_op jit(solution)/shard_map/dot_general | solution.py:109
  105.3 10.2 %all-to-all-start.3 = ((bf16[64,16,2048]{2,1,0:T(8,128)(2,1)}), bf16[64,16,2048]{2,1,0:T(8,128)(2,1)}, u32[]{:S(2)}, u32[]{:S(2)}) async-start(bf16[64,16,2048]{2,1,0:T(8,128)(2,1)} %bitcast.91), calls=%async_computation.3 | async-start | bytes 8388608 | tf_op jit(solution)/shard_map/all_to_all | solution.py:116
  116.2 5.0 %collective-permute-done = bf16[1,2048,704]{1,2,0:T(8,128)(2,1)} collective-permute-done((bf16[1,2048,704]{1,2,0:T(8,128)(2,1)}, bf16[1,2048,704]{1,2,0:T(8,128)(2,1)}, u32[]{:S(2)}, u32[]{:S(2)}) %collective-permute-start) | collective-permute-done | bytes 2883616 | tf_op jit(solution)/shard_map/ppermute | solution.py:113
  121.3 47.9 %all-to-all-done.3 = bf16[64,16,2048]{2,1,0:T(8,128)(2,1)} async-done(((bf16[64,16,2048]{2,1,0:T(8,128)(2,1)}), bf16[64,16,2048]{2,1,0:T(8,128)(2,1)}, u32[]{:S(2)}, u32[]{:S(2)}) %all-to-all-start.3) | async-done | bytes 4194336 | tf_op jit(solution)/shard_map/all_to_all | solution.py:116
  169.2 5.9 %fusion.13 = f32[1024,704]{0,1:T(8,128)S(1)} fusion(bf16[1024,2048]{1,0:T(8,128)(2,1)} %bitcast.14, bf16[1,2048,704]{1,2,0:T(8,128)(2,1)} %collective-permute-done), kind=kOutput, calls=%fused_computation.20 | convolution fusion | flops 2952790016 | bytes 9961472 | tf_op jit(solution)/shard_map/dot_general | solution.py:119
  175.1 6.6 %multiply_convert_fusion = bf16[1024,704]{0,1:T(8,128)(2,1)S(1)} fusion(f32[1024,704]{0,1:T(8,128)S(1)} %fusion.13, bf16[1024,2048]{1,0:T(8,128)(2,1)} %bitcast.14, bf16[1,2048,704]{1,2,0:T(8,128)(2,1)} %collective-permute-done.1), kind=kOutput, calls=%fused_computation.28 | convolution fusion | flops 2957115392 | bytes 11403264 | tf_op jit(solution)/shard_map/dot_general | solution.py:120
  181.7 5.1 %fusion.17 = f32[1024,704]{0,1:T(8,128)S(1)} fusion(bf16[1024,2048]{1,0:T(8,128)(2,1)} %bitcast.14, bf16[1,2048,704]{1,2,0:T(8,128)(2,1)S(1)} %copy-done.7), kind=kOutput, calls=%fused_computation.24 | convolution fusion | flops 2952790016 | bytes 9961472 | tf_op jit(solution)/shard_map/dot_general | solution.py:120
  186.9 5.9 %multiply_convert_fusion.1 = bf16[1024,704]{0,1:T(8,128)(2,1)S(1)} fusion(f32[1024,704]{0,1:T(8,128)S(1)} %fusion.17, bf16[1024,2048]{1,0:T(8,128)(2,1)} %bitcast.14, bf16[1,2048,704]{1,2,0:T(8,128)(2,1)S(1)} %copy-done.8), kind=kOutput, calls=%fused_computation.29 | convolution fusion | flops 2957115392 | bytes 11403264 | tf_op jit(solution)/shard_map/dot_general | solution.py:119
  192.8 3.7 %fusion.15 = bf16[1024,2048]{1,0:T(8,128)(2,1)S(1)} fusion(bf16[1024,704]{0,1:T(8,128)(2,1)S(1)} %multiply_convert_fusion.1, bf16[1,704,2048]{2,1,0:T(8,128)(2,1)S(1)} %copy-done.9), kind=kOutput, calls=%fused_computation.22 | convolution fusion | flops 2952790016 | bytes 8519680 | tf_op jit(solution)/shard_map/dot_general | solution.py:122
  196.5 6.8 %add_convert_fusion = bf16[1024,2048]{1,0:T(8,128)(2,1)} fusion(bf16[1024,2048]{1,0:T(8,128)(2,1)S(1)} %fusion.15, bf16[1024,704]{0,1:T(8,128)(2,1)S(1)} %multiply_convert_fusion, bf16[1,704,2048]{2,1,0:T(8,128)(2,1)} %collective-permute-done.2), kind=kOutput, calls=%fused_computation.5 | convolution fusion | flops 2963275776 | bytes 12713984 | tf_op jit(solution)/shard_map/dot_general | solution.py:122
  203.3 8.0 %all-to-all-start.4 = ((bf16[64,16,2048]{2,1,0:T(8,128)(2,1)}), bf16[64,16,2048]{2,1,0:T(8,128)(2,1)}, u32[]{:S(2)}, u32[]{:S(2)}) async-start(bf16[64,16,2048]{2,1,0:T(8,128)(2,1)} %bitcast.92), calls=%async_computation.4 | async-start | bytes 8388608 | tf_op jit(solution)/shard_map/all_to_all | solution.py:129
  212.6 52.7 %all-to-all-done.4 = bf16[64,16,2048]{2,1,0:T(8,128)(2,1)} async-done(((bf16[64,16,2048]{2,1,0:T(8,128)(2,1)}), bf16[64,16,2048]{2,1,0:T(8,128)(2,1)}, u32[]{:S(2)}, u32[]{:S(2)}) %all-to-all-start.4) | async-done | bytes 4194336 | tf_op jit(solution)/shard_map/all_to_all | solution.py:129
  265.3 5.1 %fusion.21 = bf16[128,2048]{1,0:T(8,128)(2,1)} fusion(f32[128,1024]{1,0:T(8,128)} %select_reduce_fusion, bf16[1024,2048]{1,0:T(8,128)(2,1)} %bitcast.22, bf16[128,2048]{1,0:T(8,128)(2,1)S(1)} %get-tuple-element.5, bf16[128,2048]{1,0:T(8,128)(2,1)S(1)} %copy-done.2), kind=kOutput, calls=%fused_computation.35 | convolution fusion | flops 3222536192 | bytes 6291456 | tf_op jit(solution)/shard_map/dot_general | solution.py:133
  (65 shorter events, 13.3 us)
Async XLA Ops:
  7.2 48.2 %copy-start = (bf16[16,128,512]{2,1,0:T(8,128)(2,1)S(1)}, bf16[16,128,512]{2,1,0:T(8,128)(2,1)}, u32[]{:S(2)}) copy-start(bf16[16,128,512]{2,1,0:T(8,128)(2,1)} %param.20) | copy-start | bytes 6291460
  7.2 50.3 %all-gather.4.cloned.1.call-start = ((), (), s32[]{:S(2)}) async-start(), calls=%async_computation.5 | async-start | bytes 1327104 | tf_op jit(solution)/shard_map/all_gather | solution.py:54
  20.9 28.2 %copy-start.4 = (s32[128,6]{0,1:T(8,128)S(1)}, s32[128,6]{0,1:T(8,128)}, u32[]{:S(2)}) copy-start(s32[128,6]{0,1:T(8,128)} %param.30) | copy-start | bytes 9220
  22.7 26.8 %copy-start.11 = (s32[1,4]{1,0:T(1,128)S(1)}, s32[1,4]{1,0:T(1,128)}, u32[]{:S(2)}) copy-start(s32[1,4]{1,0:T(1,128)} %param.27) | copy-start | bytes 52
  22.7 12.2 %all-to-all-start.1 = ((bf16[4,128,576]{1,2,0:T(8,128)(2,1)}), bf16[4,128,576]{1,2,0:T(8,128)(2,1)S(1)}, u32[]{:S(2)}, u32[]{:S(2)}) async-start(bf16[4,128,576]{1,2,0:T(8,128)(2,1)} %broadcast_in_dim.76), calls=%async_computation.1 | async-start | bytes 1179648 | tf_op jit(solution)/shard_map/all_to_all | solution.py:58
  36.5 11.9 %all-to-all-start.2 = ((bf16[4,128,576]{1,2,0:T(8,128)(2,1)}), bf16[4,128,576]{1,2,0:T(8,128)(2,1)S(1)}, u32[]{:S(2)}, u32[]{:S(2)}) async-start(bf16[4,128,576]{1,2,0:T(8,128)(2,1)} %broadcast_select_fusion), calls=%async_computation.2 | async-start | bytes 1179648 | tf_op jit(solution)/shard_map/all_to_all | solution.py:62
  40.0 31.5 %all-gather.6.cloned.1.call-start = ((), (), s32[]{:S(2)}) async-start(), calls=%async_computation.6 | async-start | bytes 1327104 | tf_op jit(solution)/shard_map/all_gather | solution.py:64
  71.5 16.0 %copy-start.10 = (bf16[1024,576]{0,1:T(8,128)(2,1)S(1)}, bf16[1024,576]{0,1:T(8,128)(2,1)}, u32[]{:S(2)}) copy-start(bf16[1024,576]{0,1:T(8,128)(2,1)} %all-gather.4.cloned.1.call-done) | copy-start | bytes 3538948
  87.6 9.6 %copy-start.2 = (bf16[128,2048]{1,0:T(8,128)(2,1)S(1)}, bf16[128,2048]{1,0:T(8,128)(2,1)}, u32[]{:S(2)}) copy-start(bf16[128,2048]{1,0:T(8,128)(2,1)} %param.16) | copy-start | bytes 1572868
  97.2 4.8 %copy-start.5 = (f32[2048]{0:T(1024)S(1)}, f32[2048]{0:T(1024)}, u32[]{:S(2)}) copy-start(f32[2048]{0:T(1024)} %param.23) | copy-start | bytes 24580
  102.0 163.3 %copy-start.3 = (bf16[128,2048]{1,0:T(8,128)(2,1)}, bf16[128,2048]{1,0:T(8,128)(2,1)S(1)}, u32[]{:S(2)}) copy-start(bf16[128,2048]{1,0:T(8,128)(2,1)S(1)} %get-tuple-element.5) | copy-start | bytes 1572868
  105.3 63.9 %all-to-all-start.3 = ((bf16[64,16,2048]{2,1,0:T(8,128)(2,1)}), bf16[64,16,2048]{2,1,0:T(8,128)(2,1)}, u32[]{:S(2)}, u32[]{:S(2)}) async-start(bf16[64,16,2048]{2,1,0:T(8,128)(2,1)} %bitcast.91), calls=%async_computation.3 | async-start | bytes 8388608 | tf_op jit(solution)/shard_map/all_to_all | solution.py:116
  115.6 5.7 %collective-permute-start = (bf16[1,2048,704]{1,2,0:T(8,128)(2,1)}, bf16[1,2048,704]{1,2,0:T(8,128)(2,1)}, u32[]{:S(2)}, u32[]{:S(2)}) collective-permute-start(bf16[1,2048,704]{1,2,0:T(8,128)(2,1)} %param.24), channel_id=1, source_target_pairs={{0,1},{1,0},{2,3},{3,2},{4,5},{5,4},{6,7},{7,6},{8,9},{9,8},{10,11... | collective-permute-start | bytes 8650760 | tf_op jit(solution)/shard_map/ppermute | solution.py:113
  115.7 59.4 %collective-permute-start.1 = (bf16[1,2048,704]{1,2,0:T(8,128)(2,1)}, bf16[1,2048,704]{1,2,0:T(8,128)(2,1)}, u32[]{:S(2)}, u32[]{:S(2)}) collective-permute-start(bf16[1,2048,704]{1,2,0:T(8,128)(2,1)} %param.25), channel_id=1, source_target_pairs={{0,1},{1,0},{2,3},{3,2},{4,5},{5,4},{6,7},{7,6},{8,9},{9,8},{10,11... | collective-permute-start | bytes 8650760 | tf_op jit(solution)/shard_map/ppermute | solution.py:114
  116.1 80.3 %collective-permute-start.2 = (bf16[1,704,2048]{2,1,0:T(8,128)(2,1)}, bf16[1,704,2048]{2,1,0:T(8,128)(2,1)}, u32[]{:S(2)}, u32[]{:S(2)}) collective-permute-start(bf16[1,704,2048]{2,1,0:T(8,128)(2,1)} %param.26), channel_id=1, source_target_pairs={{0,1},{1,0},{2,3},{3,2},{4,5},{5,4},{6,7},{7,6},{8,9},{9,8},{10,11... | collective-permute-start | bytes 8650760 | tf_op jit(solution)/shard_map/ppermute | solution.py:115
  175.0 6.6 %copy-start.7 = (bf16[1,2048,704]{1,2,0:T(8,128)(2,1)S(1)}, bf16[1,2048,704]{1,2,0:T(8,128)(2,1)}, u32[]{:S(2)}) copy-start(bf16[1,2048,704]{1,2,0:T(8,128)(2,1)} %param.25) | copy-start | bytes 8650756
  181.7 5.2 %copy-start.8 = (bf16[1,2048,704]{1,2,0:T(8,128)(2,1)S(1)}, bf16[1,2048,704]{1,2,0:T(8,128)(2,1)}, u32[]{:S(2)}) copy-start(bf16[1,2048,704]{1,2,0:T(8,128)(2,1)} %param.24) | copy-start | bytes 8650756
  186.9 5.9 %copy-start.9 = (bf16[1,704,2048]{2,1,0:T(8,128)(2,1)S(1)}, bf16[1,704,2048]{2,1,0:T(8,128)(2,1)}, u32[]{:S(2)}) copy-start(bf16[1,704,2048]{2,1,0:T(8,128)(2,1)} %param.26) | copy-start | bytes 8650756
  203.3 8.0 %copy-start.6 = (f32[128,6]{0,1:T(8,128)S(1)}, f32[128,6]{0,1:T(8,128)}, u32[]{:S(2)}) copy-start(f32[128,6]{0,1:T(8,128)} %param.31) | copy-start | bytes 9220
  203.3 62.0 %all-to-all-start.4 = ((bf16[64,16,2048]{2,1,0:T(8,128)(2,1)}), bf16[64,16,2048]{2,1,0:T(8,128)(2,1)}, u32[]{:S(2)}, u32[]{:S(2)}) async-start(bf16[64,16,2048]{2,1,0:T(8,128)(2,1)} %bitcast.92), calls=%async_computation.4 | async-start | bytes 8388608 | tf_op jit(solution)/shard_map/all_to_all | solution.py:129
  265.3 5.2 %copy-start.1 = (bf16[16,128,512]{2,1,0:T(8,128)(2,1)S(1)}, bf16[16,128,512]{2,1,0:T(8,128)(2,1)}, u32[]{:S(2)}) copy-start(bf16[16,128,512]{2,1,0:T(8,128)(2,1)} %param.20) | copy-start | bytes 6291460
Sparse Core Ops, SparseCore 0:
  9.7 26.0 all-gather.3
  49.2 22.2 all-gather.5

commit v5 on v4

--- a/solution.py
+++ b/solution.py
@@ -130,11 +130,10 @@
     pick_weight = jnp.sum(
         jnp.where(hits.reshape(tok_rows, top_picks, slots), gate_weights[:, :, None], 0.0), axis=1
     )
-    routed = jnp.dot(
-        pick_weight,
-        returned.astype(jnp.float32),
-        precision=lax.Precision.HIGHEST,
-        preferred_element_type=jnp.float32,
+    weight_high = pick_weight.astype(jnp.bfloat16)
+    weight_low = (pick_weight - weight_high.astype(jnp.float32)).astype(jnp.bfloat16)
+    routed = jnp.dot(weight_high, returned, preferred_element_type=jnp.float32) + jnp.dot(
+        weight_low, returned, preferred_element_type=jnp.float32
     )
     layer_out = (residual + routed).astype(jnp.bfloat16)
     return (attended, layer_out)

time: 278 us -> 280 us (level)
    dot_general x1 -> x2, matrix products: 5.15 us -> 6.93 us  [the longest x1 3.88 us: layer(): jnp.dot(weight_low, returned, preferred_element_type=jnp.float32)]
where the time goes in v5:
time: 280 us; the launch traced here: 279 us
  waiting for transfers between devices  134 us (48%)
  matrix products  77 us (28%)
  starting transfers between devices  27.2 us (10%)
  between operations  17.7 us (6%)
  blocking collectives  10.4 us (4%)
  local copies, waits for them, and re-layouts  8.22 us (3%)
  other arithmetic  4.54 us (2%)
    all_to_all x1, waiting for transfers between devices, layer(): returned = lax.all_to_all(pair_total, ('z', 'x', 'y'), 0, 0, tiled=True)  53.2 us
    all_to_all x1, waiting for transfers between devices, layer(): recv_rows = lax.all_to_all(packed, ('z', 'x', 'y'), 0, 0, tiled=True)  48 us
    sub x1, matrix products, layer(): scores - top_score  15.9 us
    all_gather x1, waiting for transfers between devices, layer(): prefix_rows = lax.all_gather(my_chunk, ('y', 'core'), axis=0, tiled=True)  14 us
    dot_general x2, matrix products, half_expert(): up_proj = jnp.dot(recv_rows, up_w, preferred_element_type=jnp.float32)  11.8 us
    dot_general x2, matrix products, half_expert(): gate_proj = jnp.dot(recv_rows, gate_w, preferred_element_type=jnp.float32)  11.7 us
    dot_general x2, matrix products, half_expert(): jnp.dot(active, down_w, preferred_element_type=jnp.float32)  10.5 us
    all_to_all x1, blocking collectives, layer(): lax.all_to_all(jnp.broadcast_to(my_slot[None], (z_count,)), 'z', 0, 0, ti...  10.4 us
  transfers between devices with their start and end apart: 9, of which 6 were waited for; matrix products, arithmetic and copies ran while one was open for 15% of the time, Pallas kernels for 0%

profile of v5, /device:TPU:2, one launch (start us, length us, event | category | flops | bytes accessed | tf_op | source)
XLA Modules:
  0.0 278.8 jit_solution(15042627016775924737)
XLA Ops:
  10.5 10.4 %all_to_all.46 = s32[4,1,1]{2,1,0:T(1,128)S(1)} all-to-all(s32[4,1,1]{2,1,0:T(1,128)S(1)} %broadcast_in_dim.74), channel_id=1, replica_groups=mesh['z'=4,'x'=4,'y'=4,'core'=2] {'z'}, dimensions={0} | all-to-all | bytes 32 | tf_op jit(solution)/shard_map/all_to_all | solution.py:55
  22.7 5.0 %all-to-all-start.1 = ((bf16[4,128,576]{1,2,0:T(8,128)(2,1)}), bf16[4,128,576]{1,2,0:T(8,128)(2,1)S(1)}, u32[]{:S(2)}, u32[]{:S(2)}) async-start(bf16[4,128,576]{1,2,0:T(8,128)(2,1)} %broadcast_in_dim.76), calls=%async_computation.1 | async-start | bytes 1179648 | tf_op jit(solution)/shard_map/all_to_all | solution.py:58
  27.8 7.1 %all-to-all-done.1 = bf16[4,128,576]{1,2,0:T(8,128)(2,1)S(1)} async-done(((bf16[4,128,576]{1,2,0:T(8,128)(2,1)}), bf16[4,128,576]{1,2,0:T(8,128)(2,1)S(1)}, u32[]{:S(2)}, u32[]{:S(2)}) %all-to-all-start.1) | async-done | bytes 589856 | tf_op jit(solution)/shard_map/all_to_all | solution.py:58
  36.5 3.5 %all-to-all-start.2 = ((bf16[4,128,576]{1,2,0:T(8,128)(2,1)}), bf16[4,128,576]{1,2,0:T(8,128)(2,1)S(1)}, u32[]{:S(2)}, u32[]{:S(2)}) async-start(bf16[4,128,576]{1,2,0:T(8,128)(2,1)} %broadcast_select_fusion), calls=%async_computation.2 | async-start | bytes 1179648 | tf_op jit(solution)/shard_map/all_to_all | solution.py:62
  42.6 5.7 %all-to-all-done.2 = bf16[4,128,576]{1,2,0:T(8,128)(2,1)S(1)} async-done(((bf16[4,128,576]{1,2,0:T(8,128)(2,1)}), bf16[4,128,576]{1,2,0:T(8,128)(2,1)S(1)}, u32[]{:S(2)}, u32[]{:S(2)}) %all-to-all-start.2) | async-done | bytes 589856 | tf_op jit(solution)/shard_map/all_to_all | solution.py:62
  55.3 2.2 convert_bitcast_fusion
  57.5 14.0 %all-gather.6.cloned.1.call-done = bf16[1,1024,576]{1,2,0:T(8,128)(2,1)} async-done(((bf16[1,128,576]{1,2,0:T(8,128)(2,1)}), bf16[1,1024,576]{1,2,0:T(8,128)(2,1)}) %all-gather.6.cloned.1.call-update) | async-done | bytes 1179664 | tf_op jit(solution)/shard_map/all_gather | solution.py:64
  71.5 15.9 %fusion.68 = (f32[128,16]{0,1:T(8,128)S(1)}, bf16[128,16,2048]{2,0,1:T(8,128)(2,1)}) fusion(pred[128,2048]{1,0:T(8,128)(4,1)S(1)} %concatenate.9, bf16[128,16,64]{0,2,1:T(8,128)(2,1)} %slice.23, bf16[128,16,512]{0,2,1:T(8,128)(2,1)} %convert_bitcast_fusion, bf16[1024,576]{0,1:T(8,128)(2,1)} %all-gather.4.cloned.1.call-done, bf16[1024,576]{0,1:T(8,128)(2,1)} %bitcast.99), kind=kOutput, calls=%fused_computation.92 | convolution fusion | flops 4866443264 | bytes 13377536 | tf_op jit(solution)/shard_map/sub | solution.py:80
  87.5 9.9 %fusion.42 = bf16[16,128,128]{1,2,0:T(8,128)(2,1)S(1)} fusion(bf16[16,512,128]{2,1,0:T(8,128)(2,1)} %param.21, bf16[128,16,2048]{2,0,1:T(8,128)(2,1)} %get-tuple-element.3, bf16[1024,576]{0,1:T(8,128)(2,1)} %bitcast.100, bf16[1024,576]{0,1:T(8,128)(2,1)} %all-gather.4.cloned.1.call-done, f32[128,16]{0,1:T(8,128)S(1)} %get-tuple-element.2), kind=kOutput, calls=%fused_computation.45 | convolution fusion | flops 4569956352 | bytes 13377536 | tf_op jit(solution)/shard_map/thc,hcv->thv/dot_general | solution.py:89
  97.4 4.8 %multiply_reduce_fusion = (f32[128]{0:T(128)S(1)}, bf16[128,2048]{1,0:T(8,128)(2,1)S(1)}) fusion(bf16[128,2048]{1,0:T(8,128)(2,1)S(1)} %copy-done.2, bf16[128,2048]{0,1:T(8,128)(2,1)S(1)} %bitcast.95, bf16[2048,2048]{1,0:T(8,128)(2,1)} %param.22), kind=kOutput, calls=%fused_computation.47 | convolution fusion | flops 1075314560 | bytes 9961984 | tf_op jit(solution)/shard_map/dot_general | solution.py:93
  102.2 3.3 %convolution_convert_fusion = bf16[1024,2048]{1,0:T(8,128)(2,1)} fusion(bf16[128,1024]{1,0:T(8,128)(2,1)S(1)} %fusion.31, bf16[128,2048]{1,0:T(8,128)(2,1)S(1)} %get-tuple-element.5, bf16[128,2048]{1,0:T(8,128)(2,1)S(1)} %copy-done.2, f32[2048]{0:T(1024)S(1)} %copy-done.6, f32[128]{0:T(128)S(1)} %add_rsqrt_fusion), kind=kOutput, calls=%fused_computation.13 | convolution fusion | flops 540540928 | bytes 5513728 | tf_op jit(solution)/shard_map/dot_general | solution.py:109
  105.5 10.3 %all-to-all-start.3 = ((bf16[64,16,2048]{2,1,0:T(8,128)(2,1)}), bf16[64,16,2048]{2,1,0:T(8,128)(2,1)}, u32[]{:S(2)}, u32[]{:S(2)}) async-start(bf16[64,16,2048]{2,1,0:T(8,128)(2,1)} %bitcast.91), calls=%async_computation.3 | async-start | bytes 8388608 | tf_op jit(solution)/shard_map/all_to_all | solution.py:116
  116.4 5.0 %collective-permute-done = bf16[1,2048,704]{1,2,0:T(8,128)(2,1)} collective-permute-done((bf16[1,2048,704]{1,2,0:T(8,128)(2,1)}, bf16[1,2048,704]{1,2,0:T(8,128)(2,1)}, u32[]{:S(2)}, u32[]{:S(2)}) %collective-permute-start) | collective-permute-done | bytes 2883616 | tf_op jit(solution)/shard_map/ppermute | solution.py:113
  121.5 48.0 %all-to-all-done.3 = bf16[64,16,2048]{2,1,0:T(8,128)(2,1)} async-done(((bf16[64,16,2048]{2,1,0:T(8,128)(2,1)}), bf16[64,16,2048]{2,1,0:T(8,128)(2,1)}, u32[]{:S(2)}, u32[]{:S(2)}) %all-to-all-start.3) | async-done | bytes 4194336 | tf_op jit(solution)/shard_map/all_to_all | solution.py:116
  169.4 5.9 %fusion.13 = f32[1024,704]{0,1:T(8,128)S(1)} fusion(bf16[1024,2048]{1,0:T(8,128)(2,1)} %bitcast.14, bf16[1,2048,704]{1,2,0:T(8,128)(2,1)} %collective-permute-done), kind=kOutput, calls=%fused_computation.20 | convolution fusion | flops 2952790016 | bytes 9961472 | tf_op jit(solution)/shard_map/dot_general | solution.py:119
  175.3 6.6 %multiply_convert_fusion = bf16[1024,704]{0,1:T(8,128)(2,1)S(1)} fusion(f32[1024,704]{0,1:T(8,128)S(1)} %fusion.13, bf16[1024,2048]{1,0:T(8,128)(2,1)} %bitcast.14, bf16[1,2048,704]{1,2,0:T(8,128)(2,1)} %collective-permute-done.1), kind=kOutput, calls=%fused_computation.28 | convolution fusion | flops 2957115392 | bytes 11403264 | tf_op jit(solution)/shard_map/dot_general | solution.py:120
  182.0 5.1 %fusion.17 = f32[1024,704]{0,1:T(8,128)S(1)} fusion(bf16[1024,2048]{1,0:T(8,128)(2,1)} %bitcast.14, bf16[1,2048,704]{1,2,0:T(8,128)(2,1)S(1)} %copy-done.8), kind=kOutput, calls=%fused_computation.24 | convolution fusion | flops 2952790016 | bytes 9961472 | tf_op jit(solution)/shard_map/dot_general | solution.py:120
  187.2 5.9 %multiply_convert_fusion.1 = bf16[1024,704]{0,1:T(8,128)(2,1)S(1)} fusion(f32[1024,704]{0,1:T(8,128)S(1)} %fusion.17, bf16[1024,2048]{1,0:T(8,128)(2,1)} %bitcast.14, bf16[1,2048,704]{1,2,0:T(8,128)(2,1)S(1)} %copy-done.9), kind=kOutput, calls=%fused_computation.29 | convolution fusion | flops 2957115392 | bytes 11403264 | tf_op jit(solution)/shard_map/dot_general | solution.py:119
  193.0 3.7 %fusion.15 = bf16[1024,2048]{1,0:T(8,128)(2,1)S(1)} fusion(bf16[1024,704]{0,1:T(8,128)(2,1)S(1)} %multiply_convert_fusion.1, bf16[1,704,2048]{2,1,0:T(8,128)(2,1)S(1)} %copy-done.10), kind=kOutput, calls=%fused_computation.22 | convolution fusion | flops 2952790016 | bytes 8519680 | tf_op jit(solution)/shard_map/dot_general | solution.py:122
  196.8 6.8 %add_convert_fusion = bf16[1024,2048]{1,0:T(8,128)(2,1)} fusion(bf16[1024,2048]{1,0:T(8,128)(2,1)S(1)} %fusion.15, bf16[1024,704]{0,1:T(8,128)(2,1)S(1)} %multiply_convert_fusion, bf16[1,704,2048]{2,1,0:T(8,128)(2,1)} %collective-permute-done.2), kind=kOutput, calls=%fused_computation.5 | convolution fusion | flops 2963275776 | bytes 12713984 | tf_op jit(solution)/shard_map/dot_general | solution.py:122
  203.6 7.7 %all-to-all-start.4 = ((bf16[64,16,2048]{2,1,0:T(8,128)(2,1)}), bf16[64,16,2048]{2,1,0:T(8,128)(2,1)}, u32[]{:S(2)}, u32[]{:S(2)}) async-start(bf16[64,16,2048]{2,1,0:T(8,128)(2,1)} %bitcast.92), calls=%async_computation.4 | async-start | bytes 8388608 | tf_op jit(solution)/shard_map/all_to_all | solution.py:129
  211.8 53.2 %all-to-all-done.4 = bf16[64,16,2048]{2,1,0:T(8,128)(2,1)} async-done(((bf16[64,16,2048]{2,1,0:T(8,128)(2,1)}), bf16[64,16,2048]{2,1,0:T(8,128)(2,1)}, u32[]{:S(2)}, u32[]{:S(2)}) %all-to-all-start.4) | async-done | bytes 4194336 | tf_op jit(solution)/shard_map/all_to_all | solution.py:129
  265.0 3.0 %fusion.55 = f32[128,2048]{1,0:T(8,128)S(1)} fusion(bf16[1024,2048]{1,0:T(8,128)(2,1)} %bitcast.22, f32[128,1024]{1,0:T(8,128)S(1)} %select_reduce_fusion), kind=kOutput, calls=%fused_computation.65 | convolution fusion | flops 537001984 | bytes 5767168 | tf_op jit(solution)/shard_map/dot_general | solution.py:135
  268.1 3.9 %fusion.22 = bf16[128,2048]{1,0:T(8,128)(2,1)} fusion(f32[128,2048]{1,0:T(8,128)S(1)} %fusion.55, bf16[1024,2048]{1,0:T(8,128)(2,1)} %bitcast.22, bf16[128,2048]{1,0:T(8,128)(2,1)S(1)} %copy-done.4, bf16[128,2048]{1,0:T(8,128)(2,1)S(1)} %copy-done.2, f32[128,1024]{1,0:T(8,128)S(1)} %select_reduce_fusion), kind=kOutput, calls=%fused_computation.36 | convolution fusion | flops 538968064 | bytes 7340032 | tf_op jit(solution)/shard_map/dot_general | solution.py:135
  (66 shorter events, 14.2 us)
Async XLA Ops:
  7.2 48.2 %copy-start = (bf16[16,128,512]{2,1,0:T(8,128)(2,1)S(1)}, bf16[16,128,512]{2,1,0:T(8,128)(2,1)}, u32[]{:S(2)}) copy-start(bf16[16,128,512]{2,1,0:T(8,128)(2,1)} %param.20) | copy-start | bytes 6291460
  7.2 50.3 %all-gather.4.cloned.1.call-start = ((), (), s32[]{:S(2)}) async-start(), calls=%async_computation.5 | async-start | bytes 1327104 | tf_op jit(solution)/shard_map/all_gather | solution.py:54
  20.9 28.2 %copy-start.5 = (s32[128,6]{0,1:T(8,128)S(1)}, s32[128,6]{0,1:T(8,128)}, u32[]{:S(2)}) copy-start(s32[128,6]{0,1:T(8,128)} %param.30) | copy-start | bytes 9220
  22.7 26.8 %copy-start.11 = (s32[1,4]{1,0:T(1,128)S(1)}, s32[1,4]{1,0:T(1,128)}, u32[]{:S(2)}) copy-start(s32[1,4]{1,0:T(1,128)} %param.27) | copy-start | bytes 52
  22.7 12.2 %all-to-all-start.1 = ((bf16[4,128,576]{1,2,0:T(8,128)(2,1)}), bf16[4,128,576]{1,2,0:T(8,128)(2,1)S(1)}, u32[]{:S(2)}, u32[]{:S(2)}) async-start(bf16[4,128,576]{1,2,0:T(8,128)(2,1)} %broadcast_in_dim.76), calls=%async_computation.1 | async-start | bytes 1179648 | tf_op jit(solution)/shard_map/all_to_all | solution.py:58
  36.5 11.9 %all-to-all-start.2 = ((bf16[4,128,576]{1,2,0:T(8,128)(2,1)}), bf16[4,128,576]{1,2,0:T(8,128)(2,1)S(1)}, u32[]{:S(2)}, u32[]{:S(2)}) async-start(bf16[4,128,576]{1,2,0:T(8,128)(2,1)} %broadcast_select_fusion), calls=%async_computation.2 | async-start | bytes 1179648 | tf_op jit(solution)/shard_map/all_to_all | solution.py:62
  40.0 31.5 %all-gather.6.cloned.1.call-start = ((), (), s32[]{:S(2)}) async-start(), calls=%async_computation.6 | async-start | bytes 1327104 | tf_op jit(solution)/shard_map/all_gather | solution.py:64
  87.5 9.9 %copy-start.2 = (bf16[128,2048]{1,0:T(8,128)(2,1)S(1)}, bf16[128,2048]{1,0:T(8,128)(2,1)}, u32[]{:S(2)}) copy-start(bf16[128,2048]{1,0:T(8,128)(2,1)} %param.16) | copy-start | bytes 1572868
  97.4 4.8 %copy-start.6 = (f32[2048]{0:T(1024)S(1)}, f32[2048]{0:T(1024)}, u32[]{:S(2)}) copy-start(f32[2048]{0:T(1024)} %param.23) | copy-start | bytes 24580
  102.1 3.3 %copy-start.3 = (bf16[128,2048]{1,0:T(8,128)(2,1)}, bf16[128,2048]{1,0:T(8,128)(2,1)S(1)}, u32[]{:S(2)}) copy-start(bf16[128,2048]{1,0:T(8,128)(2,1)S(1)} %get-tuple-element.5) | copy-start | bytes 1572868
  105.5 64.0 %all-to-all-start.3 = ((bf16[64,16,2048]{2,1,0:T(8,128)(2,1)}), bf16[64,16,2048]{2,1,0:T(8,128)(2,1)}, u32[]{:S(2)}, u32[]{:S(2)}) async-start(bf16[64,16,2048]{2,1,0:T(8,128)(2,1)} %bitcast.91), calls=%async_computation.3 | async-start | bytes 8388608 | tf_op jit(solution)/shard_map/all_to_all | solution.py:116
  115.7 5.7 %collective-permute-start = (bf16[1,2048,704]{1,2,0:T(8,128)(2,1)}, bf16[1,2048,704]{1,2,0:T(8,128)(2,1)}, u32[]{:S(2)}, u32[]{:S(2)}) collective-permute-start(bf16[1,2048,704]{1,2,0:T(8,128)(2,1)} %param.24), channel_id=1, source_target_pairs={{0,1},{1,0},{2,3},{3,2},{4,5},{5,4},{6,7},{7,6},{8,9},{9,8},{10,11... | collective-permute-start | bytes 8650760 | tf_op jit(solution)/shard_map/ppermute | solution.py:113
  115.8 59.5 %collective-permute-start.1 = (bf16[1,2048,704]{1,2,0:T(8,128)(2,1)}, bf16[1,2048,704]{1,2,0:T(8,128)(2,1)}, u32[]{:S(2)}, u32[]{:S(2)}) collective-permute-start(bf16[1,2048,704]{1,2,0:T(8,128)(2,1)} %param.25), channel_id=1, source_target_pairs={{0,1},{1,0},{2,3},{3,2},{4,5},{5,4},{6,7},{7,6},{8,9},{9,8},{10,11... | collective-permute-start | bytes 8650760 | tf_op jit(solution)/shard_map/ppermute | solution.py:114
  116.3 80.4 %collective-permute-start.2 = (bf16[1,704,2048]{2,1,0:T(8,128)(2,1)}, bf16[1,704,2048]{2,1,0:T(8,128)(2,1)}, u32[]{:S(2)}, u32[]{:S(2)}) collective-permute-start(bf16[1,704,2048]{2,1,0:T(8,128)(2,1)} %param.26), channel_id=1, source_target_pairs={{0,1},{1,0},{2,3},{3,2},{4,5},{5,4},{6,7},{7,6},{8,9},{9,8},{10,11... | collective-permute-start | bytes 8650760 | tf_op jit(solution)/shard_map/ppermute | solution.py:115
  175.3 6.6 %copy-start.8 = (bf16[1,2048,704]{1,2,0:T(8,128)(2,1)S(1)}, bf16[1,2048,704]{1,2,0:T(8,128)(2,1)}, u32[]{:S(2)}) copy-start(bf16[1,2048,704]{1,2,0:T(8,128)(2,1)} %param.25) | copy-start | bytes 8650756
  182.0 5.2 %copy-start.9 = (bf16[1,2048,704]{1,2,0:T(8,128)(2,1)S(1)}, bf16[1,2048,704]{1,2,0:T(8,128)(2,1)}, u32[]{:S(2)}) copy-start(bf16[1,2048,704]{1,2,0:T(8,128)(2,1)} %param.24) | copy-start | bytes 8650756
  187.2 5.9 %copy-start.10 = (bf16[1,704,2048]{2,1,0:T(8,128)(2,1)S(1)}, bf16[1,704,2048]{2,1,0:T(8,128)(2,1)}, u32[]{:S(2)}) copy-start(bf16[1,704,2048]{2,1,0:T(8,128)(2,1)} %param.26) | copy-start | bytes 8650756
  203.6 7.8 %copy-start.7 = (f32[128,6]{0,1:T(8,128)S(1)}, f32[128,6]{0,1:T(8,128)}, u32[]{:S(2)}) copy-start(f32[128,6]{0,1:T(8,128)} %param.31) | copy-start | bytes 9220
  203.6 61.4 %all-to-all-start.4 = ((bf16[64,16,2048]{2,1,0:T(8,128)(2,1)}), bf16[64,16,2048]{2,1,0:T(8,128)(2,1)}, u32[]{:S(2)}, u32[]{:S(2)}) async-start(bf16[64,16,2048]{2,1,0:T(8,128)(2,1)} %bitcast.92), calls=%async_computation.4 | async-start | bytes 8388608 | tf_op jit(solution)/shard_map/all_to_all | solution.py:129
  265.0 3.1 %copy-start.4 = (bf16[128,2048]{1,0:T(8,128)(2,1)S(1)}, bf16[128,2048]{1,0:T(8,128)(2,1)}, u32[]{:S(2)}) copy-start(bf16[128,2048]{1,0:T(8,128)(2,1)} %copy-done.3) | copy-start | bytes 1572868
  265.0 7.0 %copy-start.1 = (bf16[16,128,512]{2,1,0:T(8,128)(2,1)S(1)}, bf16[16,128,512]{2,1,0:T(8,128)(2,1)}, u32[]{:S(2)}) copy-start(bf16[16,128,512]{2,1,0:T(8,128)(2,1)} %param.20) | copy-start | bytes 6291460
Sparse Core Ops, SparseCore 0:
  9.7 26.0 all-gather.3
  49.2 22.2 all-gather.5

commit v6 on v4

--- a/solution.py
+++ b/solution.py
@@ -61,7 +61,10 @@
     sent = jnp.take(x_chunks, dest_slots % x_count, axis=0)
     recv_chunks = lax.all_to_all(sent, "z", 0, 0, tiled=True)
     my_chunk = lax.dynamic_index_in_dim(recv_chunks, my_slot // x_count, 0, keepdims=False)
-    prefix_rows = lax.all_gather(my_chunk, ("y", "core"), axis=0, tiled=True)
+    exp_count = lax.axis_size("y") * lax.axis_size("core")
+    prefix_rows = lax.all_to_all(
+        jnp.broadcast_to(my_chunk[None], (exp_count,) + my_chunk.shape), ("y", "core"), 0, 0, tiled=True
+    ).reshape(exp_count * my_chunk.shape[0], my_chunk.shape[1])
     key_rows = jnp.concatenate([prefix_rows, suffix_rows], axis=0)
     key_pos = jnp.arange(suffix_rows.shape[0], dtype=jnp.int32)
     key_request = request_of(key_pos, lengths)

time: 278 us -> 286 us (1.029)
  blocking collectives: 10.4 us -> 0 us
  local copies, waits for them, and re-layouts: 8.22 us -> 15.3 us
  starting transfers between devices: 27.4 us -> 33.8 us
  other arithmetic: 5.39 us -> 9.3 us
    all_gather x1 -> x0, waiting for transfers between devices: 14 us -> none  [layer(): prefix_rows = lax.all_gather(my_chunk, ('y', 'core'), axis=0, tiled=True)]
    all_to_all x0 -> x2, waiting for transfers between devices: none -> 12.6 us  [the longest x1 12.6 us: layer(): lax.all_to_all(jnp.broadcast_to(my_chunk[None], (exp_count,) + my_chunk.s...]
    all_to_all x1 -> x0, blocking collectives: 10.4 us -> none  [layer(): lax.all_to_all(jnp.broadcast_to(my_slot[None], (z_count,)), 'z', 0, 0, ti...]
    all_to_all x0 -> x2, starting transfers between devices: none -> 9.79 us  [the longest x1 5.31 us: layer(): lax.all_to_all(jnp.broadcast_to(my_slot[None], (z_count,)), 'z', 0, 0, ti...]
    all_to_all x1, starting transfers between devices: 10.2 us -> 6.49 us  [layer(): recv_rows = lax.all_to_all(packed, ('z', 'x', 'y'), 0, 0, tiled=True)]
  transfers between devices with their start and end apart: 9 -> 10, of which waited for: 6 -> 6; matrix products, arithmetic and copies ran while one was open for 15% -> 18% of each run, Pallas kernels for 0% -> 0%
where the time goes in v6:
time: 286 us; the launch traced here: 285 us
  waiting for transfers between devices  133 us (47%)
  matrix products  76.1 us (27%)
  starting transfers between devices  33.8 us (12%)
  between operations  17.8 us (6%)
  local copies, waits for them, and re-layouts  15.3 us (5%)
  other arithmetic  9.3 us (3%)
    all_to_all x1, waiting for transfers between devices, layer(): returned = lax.all_to_all(pair_total, ('z', 'x', 'y'), 0, 0, tiled=True)  52.1 us
    all_to_all x1, waiting for transfers between devices, layer(): recv_rows = lax.all_to_all(packed, ('z', 'x', 'y'), 0, 0, tiled=True)  48.4 us
    sub x1, matrix products, layer(): scores - top_score  15.8 us
    all_to_all x1, waiting for transfers between devices, layer(): lax.all_to_all(jnp.broadcast_to(my_chunk[None], (exp_count,) + my_chunk.s...  12.6 us
    dot_general x2, matrix products, half_expert(): up_proj = jnp.dot(recv_rows, up_w, preferred_element_type=jnp.float32)  11.8 us
    dot_general x2, matrix products, half_expert(): gate_proj = jnp.dot(recv_rows, gate_w, preferred_element_type=jnp.float32)  11.7 us
    dot_general x2, matrix products, half_expert(): jnp.dot(active, down_w, preferred_element_type=jnp.float32)  10.5 us
    dot_general x1, matrix products, layer(): jnp.einsum('thc,hcv->thv', latent_out, uv_weight, preferred_element_type=...  9.91 us
  transfers between devices with their start and end apart: 10, of which 6 were waited for; matrix products, arithmetic and copies ran while one was open for 18% of the time, Pallas kernels for 0%

profile of v6, /device:TPU:2, one launch (start us, length us, event | category | flops | bytes accessed | tf_op | source)
XLA Modules:
  0.0 285.2 jit_solution(16646772601150981300)
XLA Ops:
  10.4 5.3 %all-to-all-start = ((s32[4,1,1]{2,1,0:T(1,128)}), s32[4,1,1]{2,1,0:T(1,128)S(1)}, u32[]{:S(2)}, u32[]{:S(2)}) async-start(s32[4,1,1]{2,1,0:T(1,128)} %broadcast_in_dim.82), calls=%async_computation | async-start | bytes 4096 | tf_op jit(solution)/shard_map/all_to_all | solution.py:55
  27.3 4.8 %all-to-all-start.1 = ((bf16[4,128,576]{1,2,0:T(8,128)(2,1)}), bf16[4,128,576]{1,2,0:T(8,128)(2,1)S(1)}, u32[]{:S(2)}, u32[]{:S(2)}) async-start(bf16[4,128,576]{1,2,0:T(8,128)(2,1)} %broadcast_in_dim.84), calls=%async_computation.1 | async-start | bytes 1179648 | tf_op jit(solution)/shard_map/all_to_all | solution.py:58
  32.3 8.2 %all-to-all-done.1 = bf16[4,128,576]{1,2,0:T(8,128)(2,1)S(1)} async-done(((bf16[4,128,576]{1,2,0:T(8,128)(2,1)}), bf16[4,128,576]{1,2,0:T(8,128)(2,1)S(1)}, u32[]{:S(2)}, u32[]{:S(2)}) %all-to-all-start.1) | async-done | bytes 589856 | tf_op jit(solution)/shard_map/all_to_all | solution.py:58
  44.1 4.6 %all-to-all-start.2 = ((bf16[4,128,576]{1,2,0:T(8,128)(2,1)}), bf16[4,128,576]{1,2,0:T(8,128)(2,1)S(1)}, u32[]{:S(2)}, u32[]{:S(2)}) async-start(bf16[4,128,576]{1,2,0:T(8,128)(2,1)} %broadcast_select_fusion), calls=%async_computation.2 | async-start | bytes 1179648 | tf_op jit(solution)/shard_map/all_to_all | solution.py:62
  51.3 5.9 %all-to-all-done.2 = bf16[4,128,576]{1,2,0:T(8,128)(2,1)S(1)} async-done(((bf16[4,128,576]{1,2,0:T(8,128)(2,1)}), bf16[4,128,576]{1,2,0:T(8,128)(2,1)S(1)}, u32[]{:S(2)}, u32[]{:S(2)}) %all-to-all-start.2) | async-done | bytes 589856 | tf_op jit(solution)/shard_map/all_to_all | solution.py:62
  58.3 4.5 %all-to-all-start.3 = ((bf16[8,128,576]{1,2,0:T(8,128)(2,1)}), bf16[8,128,576]{1,2,0:T(8,128)(2,1)S(1)}, u32[]{:S(2)}, u32[]{:S(2)}) async-start(bf16[8,128,576]{1,2,0:T(8,128)(2,1)} %broadcast_in_dim.87), calls=%async_computation.3 | async-start | bytes 2359296 | tf_op jit(solution)/shard_map/all_to_all | solution.py:65
  64.4 3.2 %convert_bitcast_fusion = bf16[128,16,512]{0,2,1:T(8,128)(2,1)} fusion(bf16[16,128,512]{2,1,0:T(8,128)(2,1)S(1)} %copy-done, bf16[128,16,192]{0,2,1:T(8,128)(2,1)} %bitcast.103), kind=kOutput, calls=%fused_computation.38 | convolution fusion | flops 269484032 | bytes 4718592 | tf_op jit(solution)/shard_map/thn,hnc->thc/dot_general | solution.py:48
  67.5 12.6 %all-to-all-done.3 = bf16[8,128,576]{1,2,0:T(8,128)(2,1)S(1)} async-done(((bf16[8,128,576]{1,2,0:T(8,128)(2,1)}), bf16[8,128,576]{1,2,0:T(8,128)(2,1)S(1)}, u32[]{:S(2)}, u32[]{:S(2)}) %all-to-all-start.3) | async-done | bytes 1179680 | tf_op jit(solution)/shard_map/all_to_all | solution.py:65
  83.9 15.8 %fusion.56 = (f32[128,16]{0,1:T(8,128)S(1)}, bf16[128,16,2048]{2,0,1:T(8,128)(2,1)}) fusion(pred[128,2048]{1,0:T(8,128)(4,1)} %concatenate.9, bf16[2048,576]{0,1:T(8,128)(2,1)} %constant_dynamic-update-slice_fusion, bf16[128,16,64]{0,2,1:T(8,128)(2,1)} %slice.23, bf16[128,16,512]{0,2,1:T(8,128)(2,1)S(1)} %copy-done.5), kind=kOutput, calls=%fused_computation.85 | convolution fusion | flops 4861724672 | bytes 13377536 | tf_op jit(solution)/shard_map/sub | solution.py:83
  99.6 9.9 %fusion.37 = bf16[16,128,128]{1,2,0:T(8,128)(2,1)S(1)} fusion(bf16[16,512,128]{2,1,0:T(8,128)(2,1)} %param.21, bf16[128,16,2048]{2,0,1:T(8,128)(2,1)} %get-tuple-element.3, bf16[2048,576]{0,1:T(8,128)(2,1)} %constant_dynamic-update-slice_fusion, f32[128,16]{0,1:T(8,128)S(1)} %get-tuple-element.2), kind=kOutput, calls=%fused_computation.41 | convolution fusion | flops 4565762048 | bytes 13115392 | tf_op jit(solution)/shard_map/thc,hcv->thv/dot_general | solution.py:92
  109.6 4.8 %multiply_reduce_fusion = (f32[128]{0:T(128)S(1)}, bf16[128,2048]{1,0:T(8,128)(2,1)S(1)}) fusion(bf16[128,2048]{1,0:T(8,128)(2,1)S(1)} %copy-done.2, bf16[128,2048]{0,1:T(8,128)(2,1)S(1)} %bitcast.104, bf16[2048,2048]{1,0:T(8,128)(2,1)} %param.22), kind=kOutput, calls=%fused_computation.44 | convolution fusion | flops 1075314560 | bytes 9961984 | tf_op jit(solution)/shard_map/dot_general | solution.py:96
  114.4 3.3 %convolution_convert_fusion = bf16[1024,2048]{1,0:T(8,128)(2,1)} fusion(bf16[128,1024]{1,0:T(8,128)(2,1)S(1)} %fusion.33, bf16[128,2048]{1,0:T(8,128)(2,1)S(1)} %get-tuple-element.5, bf16[128,2048]{1,0:T(8,128)(2,1)S(1)} %copy-done.2, f32[2048]{0:T(1024)S(1)} %copy-done.8, f32[128]{0:T(128)S(1)} %add_rsqrt_fusion), kind=kOutput, calls=%fused_computation.13 | convolution fusion | flops 540540928 | bytes 5513728 | tf_op jit(solution)/shard_map/dot_general | solution.py:112
  117.7 6.5 %all-to-all-start.4 = ((bf16[64,16,2048]{2,1,0:T(8,128)(2,1)}), bf16[64,16,2048]{2,1,0:T(8,128)(2,1)}, u32[]{:S(2)}, u32[]{:S(2)}) async-start(bf16[64,16,2048]{2,1,0:T(8,128)(2,1)} %bitcast.100), calls=%async_computation.4 | async-start | bytes 8388608 | tf_op jit(solution)/shard_map/all_to_all | solution.py:119
  124.8 5.0 %collective-permute-done = bf16[1,2048,704]{1,2,0:T(8,128)(2,1)} collective-permute-done((bf16[1,2048,704]{1,2,0:T(8,128)(2,1)}, bf16[1,2048,704]{1,2,0:T(8,128)(2,1)}, u32[]{:S(2)}, u32[]{:S(2)}) %collective-permute-start) | collective-permute-done | bytes 2883616 | tf_op jit(solution)/shard_map/ppermute | solution.py:116
  129.9 48.4 %all-to-all-done.4 = bf16[64,16,2048]{2,1,0:T(8,128)(2,1)} async-done(((bf16[64,16,2048]{2,1,0:T(8,128)(2,1)}), bf16[64,16,2048]{2,1,0:T(8,128)(2,1)}, u32[]{:S(2)}, u32[]{:S(2)}) %all-to-all-start.4) | async-done | bytes 4194336 | tf_op jit(solution)/shard_map/all_to_all | solution.py:119
  178.3 5.9 %fusion.13 = f32[1024,704]{0,1:T(8,128)S(1)} fusion(bf16[1024,2048]{1,0:T(8,128)(2,1)} %bitcast.14, bf16[1,2048,704]{1,2,0:T(8,128)(2,1)} %collective-permute-done), kind=kOutput, calls=%fused_computation.20 | convolution fusion | flops 2952790016 | bytes 9961472 | tf_op jit(solution)/shard_map/dot_general | solution.py:122
  184.2 6.6 %multiply_convert_fusion = bf16[1024,704]{0,1:T(8,128)(2,1)S(1)} fusion(f32[1024,704]{0,1:T(8,128)S(1)} %fusion.13, bf16[1024,2048]{1,0:T(8,128)(2,1)} %bitcast.14, bf16[1,2048,704]{1,2,0:T(8,128)(2,1)} %collective-permute-done.1), kind=kOutput, calls=%fused_computation.28 | convolution fusion | flops 2957115392 | bytes 11403264 | tf_op jit(solution)/shard_map/dot_general | solution.py:123
  190.9 5.1 %fusion.17 = f32[1024,704]{0,1:T(8,128)S(1)} fusion(bf16[1024,2048]{1,0:T(8,128)(2,1)} %bitcast.14, bf16[1,2048,704]{1,2,0:T(8,128)(2,1)S(1)} %copy-done.10), kind=kOutput, calls=%fused_computation.24 | convolution fusion | flops 2952790016 | bytes 9961472 | tf_op jit(solution)/shard_map/dot_general | solution.py:123
  196.0 5.9 %multiply_convert_fusion.1 = bf16[1024,704]{0,1:T(8,128)(2,1)S(1)} fusion(f32[1024,704]{0,1:T(8,128)S(1)} %fusion.17, bf16[1024,2048]{1,0:T(8,128)(2,1)} %bitcast.14, bf16[1,2048,704]{1,2,0:T(8,128)(2,1)S(1)} %copy-done.11), kind=kOutput, calls=%fused_computation.29 | convolution fusion | flops 2957115392 | bytes 11403264 | tf_op jit(solution)/shard_map/dot_general | solution.py:122
  201.9 3.7 %fusion.15 = bf16[1024,2048]{1,0:T(8,128)(2,1)S(1)} fusion(bf16[1024,704]{0,1:T(8,128)(2,1)S(1)} %multiply_convert_fusion.1, bf16[1,704,2048]{2,1,0:T(8,128)(2,1)S(1)} %copy-done.12), kind=kOutput, calls=%fused_computation.22 | convolution fusion | flops 2952790016 | bytes 8519680 | tf_op jit(solution)/shard_map/dot_general | solution.py:125
  205.6 6.8 %add_convert_fusion = bf16[1024,2048]{1,0:T(8,128)(2,1)} fusion(bf16[1024,2048]{1,0:T(8,128)(2,1)S(1)} %fusion.15, bf16[1024,704]{0,1:T(8,128)(2,1)S(1)} %multiply_convert_fusion, bf16[1,704,2048]{2,1,0:T(8,128)(2,1)} %collective-permute-done.2), kind=kOutput, calls=%fused_computation.5 | convolution fusion | flops 2963275776 | bytes 12713984 | tf_op jit(solution)/shard_map/dot_general | solution.py:125
  212.5 7.4 %all-to-all-start.5 = ((bf16[64,16,2048]{2,1,0:T(8,128)(2,1)}), bf16[64,16,2048]{2,1,0:T(8,128)(2,1)}, u32[]{:S(2)}, u32[]{:S(2)}) async-start(bf16[64,16,2048]{2,1,0:T(8,128)(2,1)} %bitcast.101), calls=%async_computation.5 | async-start | bytes 8388608 | tf_op jit(solution)/shard_map/all_to_all | solution.py:132
  221.1 52.1 %all-to-all-done.5 = bf16[64,16,2048]{2,1,0:T(8,128)(2,1)} async-done(((bf16[64,16,2048]{2,1,0:T(8,128)(2,1)}), bf16[64,16,2048]{2,1,0:T(8,128)(2,1)}, u32[]{:S(2)}, u32[]{:S(2)}) %all-to-all-start.5) | async-done | bytes 4194336 | tf_op jit(solution)/shard_map/all_to_all | solution.py:132
  273.3 5.1 %fusion.21 = bf16[128,2048]{1,0:T(8,128)(2,1)} fusion(f32[128,1024]{1,0:T(8,128)} %select_reduce_fusion, bf16[1024,2048]{1,0:T(8,128)(2,1)} %bitcast.22, bf16[128,2048]{1,0:T(8,128)(2,1)S(1)} %get-tuple-element.5, bf16[128,2048]{1,0:T(8,128)(2,1)S(1)} %copy-done.2), kind=kOutput, calls=%fused_computation.32 | convolution fusion | flops 3222536192 | bytes 6291456 | tf_op jit(solution)/shard_map/dot_general | solution.py:136
  (70 shorter events, 26.0 us)
Async XLA Ops:
  7.2 57.2 %copy-start = (bf16[16,128,512]{2,1,0:T(8,128)(2,1)S(1)}, bf16[16,128,512]{2,1,0:T(8,128)(2,1)}, u32[]{:S(2)}) copy-start(bf16[16,128,512]{2,1,0:T(8,128)(2,1)} %param.20) | copy-start | bytes 6291460
  7.2 19.2 %copy-start.6 = (bf16[128,576]{0,1:T(8,128)(2,1)S(1)}, bf16[128,576]{0,1:T(8,128)(2,1)}, u32[]{:S(2)}) copy-start(bf16[128,576]{0,1:T(8,128)(2,1)} %param.19) | copy-start | bytes 442372
  10.4 16.0 %all-to-all-start = ((s32[4,1,1]{2,1,0:T(1,128)}), s32[4,1,1]{2,1,0:T(1,128)S(1)}, u32[]{:S(2)}, u32[]{:S(2)}) async-start(s32[4,1,1]{2,1,0:T(1,128)} %broadcast_in_dim.82), calls=%async_computation | async-start | bytes 4096 | tf_op jit(solution)/shard_map/all_to_all | solution.py:55
  15.7 65.7 %all-gather.2.cloned.1.call-start = ((), (), s32[]{:S(2)}) async-start(), calls=%async_computation.6 | async-start | bytes 1327104 | tf_op jit(solution)/shard_map/all_gather | solution.py:54
  22.5 21.6 %copy-start.4 = (bf16[128,3072]{0,1:T(8,128)(2,1)}, bf16[128,3072]{0,1:T(8,128)(2,1)S(1)}, u32[]{:S(2)}) copy-start(bf16[128,3072]{0,1:T(8,128)(2,1)S(1)} %copy.66) | copy-start | bytes 2359300
  27.3 13.3 %all-to-all-start.1 = ((bf16[4,128,576]{1,2,0:T(8,128)(2,1)}), bf16[4,128,576]{1,2,0:T(8,128)(2,1)S(1)}, u32[]{:S(2)}, u32[]{:S(2)}) async-start(bf16[4,128,576]{1,2,0:T(8,128)(2,1)} %broadcast_in_dim.84), calls=%async_computation.1 | async-start | bytes 1179648 | tf_op jit(solution)/shard_map/all_to_all | solution.py:58
  44.1 19.8 %copy-start.7 = (s32[128,6]{0,1:T(8,128)S(1)}, s32[128,6]{0,1:T(8,128)}, u32[]{:S(2)}) copy-start(s32[128,6]{0,1:T(8,128)} %param.30) | copy-start | bytes 9220
  44.1 13.1 %all-to-all-start.2 = ((bf16[4,128,576]{1,2,0:T(8,128)(2,1)}), bf16[4,128,576]{1,2,0:T(8,128)(2,1)S(1)}, u32[]{:S(2)}, u32[]{:S(2)}) async-start(bf16[4,128,576]{1,2,0:T(8,128)(2,1)} %broadcast_select_fusion), calls=%async_computation.2 | async-start | bytes 1179648 | tf_op jit(solution)/shard_map/all_to_all | solution.py:62
  58.3 21.8 %all-to-all-start.3 = ((bf16[8,128,576]{1,2,0:T(8,128)(2,1)}), bf16[8,128,576]{1,2,0:T(8,128)(2,1)S(1)}, u32[]{:S(2)}, u32[]{:S(2)}) async-start(bf16[8,128,576]{1,2,0:T(8,128)(2,1)} %broadcast_in_dim.87), calls=%async_computation.3 | async-start | bytes 2359296 | tf_op jit(solution)/shard_map/all_to_all | solution.py:65
  67.5 16.3 %copy-start.5 = (bf16[128,16,512]{0,2,1:T(8,128)(2,1)S(1)}, bf16[128,16,512]{0,2,1:T(8,128)(2,1)}, u32[]{:S(2)}) copy-start(bf16[128,16,512]{0,2,1:T(8,128)(2,1)} %convert_bitcast_fusion) | copy-start | bytes 6291460
  99.6 9.9 %copy-start.2 = (bf16[128,2048]{1,0:T(8,128)(2,1)S(1)}, bf16[128,2048]{1,0:T(8,128)(2,1)}, u32[]{:S(2)}) copy-start(bf16[128,2048]{1,0:T(8,128)(2,1)} %param.16) | copy-start | bytes 1572868
  109.5 4.8 %copy-start.8 = (f32[2048]{0:T(1024)S(1)}, f32[2048]{0:T(1024)}, u32[]{:S(2)}) copy-start(f32[2048]{0:T(1024)} %param.23) | copy-start | bytes 24580
  114.3 158.9 %copy-start.3 = (bf16[128,2048]{1,0:T(8,128)(2,1)}, bf16[128,2048]{1,0:T(8,128)(2,1)S(1)}, u32[]{:S(2)}) copy-start(bf16[128,2048]{1,0:T(8,128)(2,1)S(1)} %get-tuple-element.5) | copy-start | bytes 1572868
  117.7 60.6 %all-to-all-start.4 = ((bf16[64,16,2048]{2,1,0:T(8,128)(2,1)}), bf16[64,16,2048]{2,1,0:T(8,128)(2,1)}, u32[]{:S(2)}, u32[]{:S(2)}) async-start(bf16[64,16,2048]{2,1,0:T(8,128)(2,1)} %bitcast.100), calls=%async_computation.4 | async-start | bytes 8388608 | tf_op jit(solution)/shard_map/all_to_all | solution.py:119
  124.2 5.7 %collective-permute-start = (bf16[1,2048,704]{1,2,0:T(8,128)(2,1)}, bf16[1,2048,704]{1,2,0:T(8,128)(2,1)}, u32[]{:S(2)}, u32[]{:S(2)}) collective-permute-start(bf16[1,2048,704]{1,2,0:T(8,128)(2,1)} %param.24), channel_id=1, source_target_pairs={{0,1},{1,0},{2,3},{3,2},{4,5},{5,4},{6,7},{7,6},{8,9},{9,8},{10,11... | collective-permute-start | bytes 8650760 | tf_op jit(solution)/shard_map/ppermute | solution.py:116
  124.2 60.0 %collective-permute-start.1 = (bf16[1,2048,704]{1,2,0:T(8,128)(2,1)}, bf16[1,2048,704]{1,2,0:T(8,128)(2,1)}, u32[]{:S(2)}, u32[]{:S(2)}) collective-permute-start(bf16[1,2048,704]{1,2,0:T(8,128)(2,1)} %param.25), channel_id=1, source_target_pairs={{0,1},{1,0},{2,3},{3,2},{4,5},{5,4},{6,7},{7,6},{8,9},{9,8},{10,11... | collective-permute-start | bytes 8650760 | tf_op jit(solution)/shard_map/ppermute | solution.py:117
  124.7 80.9 %collective-permute-start.2 = (bf16[1,704,2048]{2,1,0:T(8,128)(2,1)}, bf16[1,704,2048]{2,1,0:T(8,128)(2,1)}, u32[]{:S(2)}, u32[]{:S(2)}) collective-permute-start(bf16[1,704,2048]{2,1,0:T(8,128)(2,1)} %param.26), channel_id=1, source_target_pairs={{0,1},{1,0},{2,3},{3,2},{4,5},{5,4},{6,7},{7,6},{8,9},{9,8},{10,11... | collective-permute-start | bytes 8650760 | tf_op jit(solution)/shard_map/ppermute | solution.py:118
  184.2 6.6 %copy-start.10 = (bf16[1,2048,704]{1,2,0:T(8,128)(2,1)S(1)}, bf16[1,2048,704]{1,2,0:T(8,128)(2,1)}, u32[]{:S(2)}) copy-start(bf16[1,2048,704]{1,2,0:T(8,128)(2,1)} %param.25) | copy-start | bytes 8650756
  190.8 5.2 %copy-start.11 = (bf16[1,2048,704]{1,2,0:T(8,128)(2,1)S(1)}, bf16[1,2048,704]{1,2,0:T(8,128)(2,1)}, u32[]{:S(2)}) copy-start(bf16[1,2048,704]{1,2,0:T(8,128)(2,1)} %param.24) | copy-start | bytes 8650756
  196.0 5.9 %copy-start.12 = (bf16[1,704,2048]{2,1,0:T(8,128)(2,1)S(1)}, bf16[1,704,2048]{2,1,0:T(8,128)(2,1)}, u32[]{:S(2)}) copy-start(bf16[1,704,2048]{2,1,0:T(8,128)(2,1)} %param.26) | copy-start | bytes 8650756
  212.5 7.4 %copy-start.9 = (f32[128,6]{0,1:T(8,128)S(1)}, f32[128,6]{0,1:T(8,128)}, u32[]{:S(2)}) copy-start(f32[128,6]{0,1:T(8,128)} %param.31) | copy-start | bytes 9220
  212.5 60.8 %all-to-all-start.5 = ((bf16[64,16,2048]{2,1,0:T(8,128)(2,1)}), bf16[64,16,2048]{2,1,0:T(8,128)(2,1)}, u32[]{:S(2)}, u32[]{:S(2)}) async-start(bf16[64,16,2048]{2,1,0:T(8,128)(2,1)} %bitcast.101), calls=%async_computation.5 | async-start | bytes 8388608 | tf_op jit(solution)/shard_map/all_to_all | solution.py:132
  273.2 5.2 %copy-start.1 = (bf16[16,128,512]{2,1,0:T(8,128)(2,1)S(1)}, bf16[16,128,512]{2,1,0:T(8,128)(2,1)}, u32[]{:S(2)}) copy-start(bf16[16,128,512]{2,1,0:T(8,128)(2,1)} %param.20) | copy-start | bytes 6291460
Sparse Core Ops, SparseCore 0:
  18.2 25.5 all-gather.1
